TPU v7x, 128 devices: a whole 4x4x4 slice. The times are simulated.
128 devices in a mesh: gx: 32 (over y_hi, x, z), gy: 4 (over y_lo, core).
Axes of the slice: x: 4, y: 4 (y_hi: 2, y_lo: 2; y = y_hi * 2 + y_lo), z: 4, core: 2. Of those that a mesh axis runs over, the one named last changes fastest.
Arguments:
- volume: bfloat16 [16, 128, 32, 256], P(None, 'gx', 'gy'), may hold values from -6 to 6
- fine_kernel: bfloat16 [3, 3, 3, 16, 16], replicated, may hold values from -0.3125 to 0.3125
- coarse_kernel: bfloat16 [3, 3, 3, 32, 16], replicated, may hold values from -0.3125 to 0.3125
- fine_cotangent: bfloat16 [16, 128, 32, 256], P(None, 'gx', 'gy'), may hold values from -6 to 6
- coarse_cotangent: bfloat16 [32, 64, 16, 128], P(None, 'gx', 'gy'), may hold values from -18 to 18
Outputs:
- fine_out: bfloat16 [16, 128, 32, 256], P(None, 'gx', 'gy')
- coarse_out: bfloat16 [32, 64, 16, 128], P(None, 'gx', 'gy')
- volume_grad: bfloat16 [16, 128, 32, 256], P(None, 'gx', 'gy')
- fine_kernel_grad: float32 [3, 3, 3, 16, 16], replicated
- coarse_kernel_grad: float32 [3, 3, 3, 32, 16], replicated
All inputs are finite; a program needn't handle non-finite values.
Results may differ from a plain program's by a relative error of at most 0.0064.
Values may be sent and summed in bfloat16 or wider, within the bound.
A program may use at most 64 MiB of HBM per device.

v0:
```python
import jax
import jax.numpy as jnp
from jax import lax
from jax.sharding import Mesh
from jax.sharding import PartitionSpec as P

GY = ("gy_0", "gy_1")
GX_GY = ("gx", "gy_0", "gy_1")


def with_halo(block, sides, width):
    for axis, dim in sides:
        count = lax.axis_size(axis)
        forward = [(i, i + 1) for i in range(count - 1)]
        backward = [(target, source) for source, target in forward]
        low = lax.ppermute(
            lax.slice_in_dim(block, block.shape[dim] - width, None, axis=dim), axis, forward
        )
        high = lax.ppermute(lax.slice_in_dim(block, 0, width, axis=dim), axis, backward)
        block = jnp.concatenate([low, block, high], axis=dim)
    return block


def copy_for_each(value, axis):
    copies = jnp.broadcast_to(value, (lax.axis_size(axis), *value.shape))
    return lax.all_to_all(copies, axis, split_axis=0, concat_axis=0, tiled=True)


def laid_out(tiles, dim):
    tiles = jnp.moveaxis(tiles, 0, dim)
    dims = tiles.shape
    return tiles.reshape(*dims[:dim], dims[dim] * dims[dim + 1], *dims[dim + 2 :])


def gather_directly(value, axis, dim):
    tiles = copy_for_each(value, axis)
    return laid_out(tiles, dim)


def cut_along(value, dim, length):
    dims = value.shape
    tiles = value.reshape(*dims[:dim], length, dims[dim] // length, *dims[dim + 1 :])
    return jnp.moveaxis(tiles, dim, 0)


def moved_by_axis(tiles, axes, turns):
    inside = tiles.shape[1:]
    whole = tiles.reshape(*(lax.axis_size(a) for a in axes), *inside)
    for k in turns:
        whole = lax.all_to_all(whole, axes[k], k, k, tiled=True)
    return whole.reshape(-1, *inside)


def core_and_chips(value, groups, turns, split_dim, concat_dim):
    length = lax.axis_size(groups[0]) * lax.axis_size(groups[1])
    tiles = cut_along(value, split_dim, length)
    return laid_out(moved_by_axis(tiles, groups, turns), concat_dim)


def silu_slope(values):
    sigma = jax.nn.sigmoid(values)
    return sigma * (1.0 + values * (1.0 - sigma))


def correlate(padded, weights, flipped, depth_cells, row_count, width_cells):
    summed = None
    for shift_z in range(3):
        for shift_y in range(3):
            for shift_x in range(3):
                if flipped:
                    matrix = weights[shift_z, shift_y, shift_x].T
                    start_z, start_y, start_x = (2 - shift_z, 2 - shift_y, 2 - shift_x)
                else:
                    matrix = weights[shift_z, shift_y, shift_x]
                    start_z, start_y, start_x = (shift_z, shift_y, shift_x)
                piece = padded[
                    :,
                    start_z : start_z + depth_cells,
                    start_y : start_y + row_count,
                    start_x : start_x + width_cells,
                ]
                piece = piece.reshape(padded.shape[0], -1)
                contrib = jnp.dot(matrix, piece, preferred_element_type=jnp.float32)
                summed = contrib if summed is None else summed + contrib
    return summed.reshape(-1, depth_cells, row_count, width_cells)


def kernel_terms(slope, padded):
    depth_cells, row_count, width_cells = slope.shape[1:]
    flat_slope = slope.reshape(slope.shape[0], -1)
    stacked = []
    for shift_z in range(3):
        for shift_y in range(3):
            for shift_x in range(3):
                piece = padded[
                    :,
                    shift_z : shift_z + depth_cells,
                    shift_y : shift_y + row_count,
                    shift_x : shift_x + width_cells,
                ]
                piece = piece.reshape(padded.shape[0], -1)
                stacked.append(
                    lax.dot_general(
                        flat_slope,
                        piece,
                        (((1,), (1,)), ((), ())),
                        preferred_element_type=jnp.float32,
                    )
                )
    return jnp.stack(stacked).reshape(3, 3, 3, slope.shape[0], padded.shape[0])


def pool_mean(values):
    chans, depth_cells, row_count, width_cells = values.shape
    blocks = values.astype(jnp.float32).reshape(
        chans, depth_cells // 2, 2, row_count // 2, 2, width_cells // 2, 2
    )
    return blocks.mean(axis=(2, 4, 6))


def spread_cells(grads):
    chans, depth_cells, row_count, width_cells = grads.shape
    wide = jnp.broadcast_to(
        grads[:, :, None, :, None, :, None], (chans, depth_cells, 2, row_count, 2, width_cells, 2)
    )
    return wide.reshape(chans, 2 * depth_cells, 2 * row_count, 2 * width_cells) / 8.0


def pad_width(values):
    return jnp.pad(values, ((0, 0), (0, 0), (0, 0), (1, 1)))


def pad_rows_width(values):
    return jnp.pad(values, ((0, 0), (0, 0), (1, 1), (1, 1)))


def local(volume, fine_kernel, coarse_kernel, fine_cotangent, coarse_cotangent):
    depth_cells, row_count, width_cells = volume.shape[1:]
    half_depth, half_rows, half_width = (depth_cells // 2, row_count // 2, width_cells // 2)
    total_cells = depth_cells * lax.axis_size("gx") * row_count * lax.axis_size(GY) * width_cells
    padded = pad_width(with_halo(volume, (("gx", 1), (GY, 2)), 1))
    fine_pre = correlate(padded, fine_kernel, False, depth_cells, row_count, width_cells)
    fine_out = (volume.astype(jnp.float32) + jax.nn.silu(fine_pre)).astype(jnp.bfloat16)
    pooled = pool_mean(fine_out).astype(jnp.bfloat16)
    all_rows = gather_directly(pooled, GY, 2)
    full_rows = all_rows.shape[2]
    coarse_pad = pad_rows_width(with_halo(all_rows, (("gx", 1),), 1))
    group_size = coarse_kernel.shape[3] // lax.axis_size(GY)
    first_channel = lax.axis_index(GY) * group_size
    kernel_part = lax.dynamic_slice_in_dim(coarse_kernel, first_channel, group_size, 3)
    coarse_pre = correlate(coarse_pad, kernel_part, False, half_depth, full_rows, half_width)
    coarse_part = jax.nn.silu(coarse_pre).astype(jnp.bfloat16)
    coarse_out = core_and_chips(coarse_part, ("gy_0", "gy_1"), (1, 0), 2, 0)
    cot_part = lax.all_to_all(coarse_cotangent, GY, split_axis=0, concat_axis=2, tiled=True)
    coarse_slope = (cot_part.astype(jnp.float32) * silu_slope(coarse_pre)).astype(jnp.bfloat16)
    slope_pad = pad_rows_width(with_halo(coarse_slope, (("gx", 1),), 1))
    grad_terms = correlate(slope_pad, kernel_part, True, half_depth, full_rows, half_width)
    pooled_grad = lax.psum_scatter(grad_terms, GY, scatter_dimension=2, tiled=True)
    partial_kernel = kernel_terms(coarse_slope, coarse_pad)
    coarse_terms = lax.dynamic_update_slice_in_dim(
        jnp.zeros(coarse_kernel.shape, jnp.float32), partial_kernel, first_channel, 3
    )
    fine_grad = fine_cotangent.astype(jnp.float32) + spread_cells(pooled_grad)
    fine_slope = (fine_grad * silu_slope(fine_pre)).astype(jnp.bfloat16)
    fine_slope_pad = pad_width(with_halo(fine_slope, (("gx", 1), (GY, 2)), 1))
    volume_grad = (
        fine_grad
        + correlate(fine_slope_pad, fine_kernel, True, depth_cells, row_count, width_cells)
    ).astype(jnp.bfloat16)
    fine_terms = kernel_terms(fine_slope, padded)
    fine_summed, coarse_summed = lax.psum((fine_terms, coarse_terms), GX_GY)
    fine_kernel_grad = fine_summed * total_cells ** (-0.5)
    coarse_kernel_grad = coarse_summed * (total_cells // 8) ** (-0.5)
    return (fine_out, coarse_out, volume_grad, fine_kernel_grad, coarse_kernel_grad)


def solution(mesh):
    torus = Mesh(mesh.devices.reshape(mesh.shape["gx"], 2, 2), ("gx", "gy_0", "gy_1"))
    placed = (P(None, "gx", GY, None), P(), P(), P(None, "gx", GY, None), P(None, "gx", GY, None))
    return jax.shard_map(
        local,
        mesh=torus,
        in_specs=placed,
        out_specs=(
            P(None, "gx", GY, None),
            P(None, "gx", GY, None),
            P(None, "gx", GY, None),
            P(),
            P(),
        ),
        check_vma=False,
    )
```

profile of v0, /device:TPU:1, one launch (start us, length us, event | category | flops | bytes accessed | tf_op | source)
XLA Modules:
  0.0 323.6 jit_solution(4583060354507611674)
XLA Ops:
  7.2 1.2 copy.860
  8.4 4.4 %collective-permute-start = (bf16[16,1,8,256]{3,0,2,1:T(8,128)(2,1)S(1)}, bf16[16,1,8,256]{3,0,2,1:T(8,128)(2,1)S(1)}, u32[]{:S(2)}, u32[]{:S(2)}) collective-permute-start(bf16[16,1,8,256]{3,0,2,1:T(8,128)(2,1)S(1)} %get-tuple-element.159), channel_id=1, source_target_pairs={{0,4},{4,8},{8,12},{12,16},{16,20},{20,24},{24,28},{28,32},{32,36}... | collective-permute-start | bytes 196616 | tf_op jit(solution)/shard_map/ppermute | solution.py:16
  12.7 1.3 collective-permute-start.1
  16.2 1.7 collective-permute-done.1
  18.0 5.0 %collective-permute-start.2 = (bf16[16,6,1,256]{3,0,2,1:T(8,128)(2,1)S(1)}, bf16[16,6,1,256]{3,0,2,1:T(8,128)(2,1)S(1)}, u32[]{:S(2)}, u32[]{:S(2)}) collective-permute-start(bf16[16,6,1,256]{3,0,2,1:T(8,128)(2,1)S(1)} %get-tuple-element.126), channel_id=1, source_target_pairs={{0,1},{1,2},{2,3},{4,5},{5,6},{6,7},{8,9},{9,10},{10,11},{12,13},{... | collective-permute-start | bytes 147464 | tf_op jit(solution)/shard_map/ppermute | solution.py:16
  23.0 1.9 collective-permute-start.3
  25.0 3.4 %collective-permute-done.3 = bf16[16,6,1,256]{3,0,2,1:T(8,128)(2,1)S(1)} collective-permute-done((bf16[16,6,1,256]{3,0,2,1:T(8,128)(2,1)S(1)}, bf16[16,6,1,256]{3,0,2,1:T(8,128)(2,1)S(1)}, u32[]{:S(2)}, u32[]{:S(2)}) %collective-permute-start.3) | collective-permute-done | bytes 49184 | tf_op jit(solution)/shard_map/ppermute | solution.py:19
  37.0 2.5 copy.892
  39.5 5.0 %reduce_sum.9 = f32[16,2,4,128]{0,3,2,1:T(8,128)S(1)} reduce(f32[16,2,2,4,2,128,2]{0,6,5,4,3,2,1:T(2,128)} %bitcast.1353, f32[]{:T(128)} %constant.10.clone.1), dimensions={2,4,6}, to_apply=%region_0.1 | reduce | flops 114688 | bytes 589828 | tf_op jit(solution)/shard_map/reduce_sum | solution.py:118
  45.3 3.3 %all-to-all-start = ((bf16[4,16,2,4,128]{4,1,3,2,0:T(8,128)(2,1)}), bf16[4,16,2,4,128]{4,1,3,2,0:T(8,128)(2,1)S(1)}, u32[]{:S(2)}, u32[]{:S(2)}) async-start(bf16[4,16,2,4,128]{4,1,3,2,0:T(8,128)(2,1)} %broadcast_in_dim.12), calls=%async_computation | async-start | bytes 262144 | tf_op jit(solution)/shard_map/all_to_all | solution.py:26
  48.7 2.0 all-to-all-done
  50.7 4.3 %all-to-all-start.3 = ((bf16[32,2,4,128]{3,2,1,0:T(4,128)(2,1)}), bf16[32,2,4,128]{3,2,1,0:T(4,128)(2,1)S(1)}, u32[]{:S(2)}, u32[]{:S(2)}) async-start(bf16[32,2,4,128]{3,2,1,0:T(4,128)(2,1)} %param.9), calls=%async_computation.3 | async-start | bytes 131072 | tf_op jit(solution)/shard_map/all_to_all | solution.py:154
  55.0 3.5 %collective-permute-start.4 = (bf16[16,1,16,128]{3,0,2,1:T(8,128)(2,1)S(1)}, bf16[16,1,16,128]{3,0,2,1:T(8,128)(2,1)S(1)}, u32[]{:S(2)}, u32[]{:S(2)}) collective-permute-start(bf16[16,1,16,128]{3,0,2,1:T(8,128)(2,1)S(1)} %get-tuple-element.164), channel_id=1, source_target_pairs={{0,4},{4,8},{8,12},{12,16},{16,20},{20,24},{24,28},{28,32},{32,36}... | collective-permute-start | bytes 196616 | tf_op jit(solution)/shard_map/ppermute | solution.py:16
  58.6 1.5 collective-permute-start.5
  60.3 3.4 %collective-permute-done.5 = bf16[16,1,16,128]{3,0,2,1:T(8,128)(2,1)} collective-permute-done((bf16[16,1,16,128]{3,0,2,1:T(8,128)(2,1)S(1)}, bf16[16,1,16,128]{3,0,2,1:T(8,128)(2,1)}, u32[]{:S(2)}, u32[]{:S(2)}) %collective-permute-start.5) | collective-permute-done | bytes 65568 | tf_op jit(solution)/shard_map/ppermute | solution.py:19
  80.0 4.2 %collective-permute-start.6 = (bf16[8,1,16,128]{3,0,2,1:T(8,128)(2,1)S(1)}, bf16[8,1,16,128]{3,0,2,1:T(8,128)(2,1)S(1)}, u32[]{:S(2)}, u32[]{:S(2)}) collective-permute-start(bf16[8,1,16,128]{3,0,2,1:T(8,128)(2,1)S(1)} %get-tuple-element.170), channel_id=1, source_target_pairs={{0,4},{4,8},{8,12},{12,16},{16,20},{20,24},{24,28},{28,32},{32,36}... | collective-permute-start | bytes 98312 | tf_op jit(solution)/shard_map/ppermute | solution.py:16
  84.2 1.3 collective-permute-start.7
  85.7 3.1 collective-permute-done.7
  97.1 5.8 %all_to_all.24 = bf16[2,2,8,2,4,128]{5,4,3,2,0,1:T(4,128)(2,1)S(1)} all-to-all(bf16[2,2,8,2,4,128]{5,4,3,2,0,1:T(4,128)(2,1)S(1)} %copy.924), channel_id=1, replica_groups=mesh['gx'=32,'gy_0'=2,'gy_1'=2] {'gy_1'}, dimensions={1} | all-to-all | bytes 131072 | tf_op jit(solution)/shard_map/all_to_all | solution.py:50
  103.6 3.3 %all-to-all-start.2 = ((bf16[2,2,8,2,4,128]{5,2,1,4,3,0:T(8,128)(2,1)}), bf16[2,2,8,2,4,128]{5,2,1,4,3,0:T(8,128)(2,1)S(1)}, u32[]{:S(2)}, u32[]{:S(2)}) async-start(bf16[2,2,8,2,4,128]{5,2,1,4,3,0:T(8,128)(2,1)} %copy.925), calls=%async_computation.2 | async-start | bytes 131072 | tf_op jit(solution)/shard_map/all_to_all | solution.py:50
  107.8 4.1 %dynamic_update_slice.3 = f32[3,3,3,32,16]{3,4,2,1,0:T(8,128)S(1)} dynamic-update-slice(f32[3,3,3,32,16]{3,4,2,1,0:T(8,128)S(1)} %broadcast_in_dim.14, f32[3,3,3,8,16]{3,4,2,1,0:T(8,128)S(1)} %copy.996, s32[]{:T(128)} %constant.13.clone.1, s32[]{:T(128)} %constant.13.clone.1, s32[]{:T(128)} %constant.13.clone.1, s32[]{:T(128)S(6)} %select_n.4, s32[]{:T(128)} %constant.13.clone.1) | dynamic-update-slice | bytes 27652 | tf_op jit(solution)/shard_map/dynamic_update_slice | solution.py:160
  112.6 17.2 %reduce-scatter.2.cloned.1.call-done = f32[16,2,4,128]{3,0,1,2:T(8,128)} async-done(((f32[16,2,16,128]{3,0,1,2:T(8,128)}), f32[16,2,4,128]{3,0,1,2:T(8,128)}) %reduce-scatter.2.cloned.1.call-update) | async-done | bytes 65552 | tf_op jit(solution)/shard_map/reduce_scatter | solution.py:158
  130.9 3.9 %broadcast_in_dim.13 = f32[16,2,2,4,2,128,2]{0,6,5,4,3,2,1:T(2,128)} broadcast(f32[16,2,4,128]{0,3,2,1:T(8,128)S(1)} %copy.933), dimensions={0,1,3,5} | broadcast | bytes 589824 | tf_op jit(solution)/shard_map/broadcast_in_dim | solution.py:123
  134.8 2.9 copy.934
  147.3 3.2 collective-permute-start.8
  150.5 1.3 collective-permute-start.9
  151.9 140.9 %all-reduce.7.cloned.1.call-done = (f32[3,3,3,16,16]{4,3,2,1,0:T(8,128)}, f32[3,3,3,32,16]{3,4,2,1,0:T(8,128)}) async-done(((f32[3,3,3,16,16]{4,3,2,1,0:T(8,128)}, f32[3,3,3,32,16]{3,4,2,1,0:T(8,128)}), (f32[3,3,3,16,16]{4,3,2,1,0:T(8,128)}, f32[3,3,3,32,16]{3,4,2,1,0:T(8,128)})) %all-reduce.7.cloned.1.call-update) | async-done | bytes 82960 | tf_op jit(solution)/shard_map/psum | solution.py:171
  292.8 1.6 broadcast_multiply_fusion
  294.4 1.6 broadcast_multiply_fusion.1
  296.3 3.7 %collective-permute-start.10 = (bf16[16,6,1,256]{3,2,1,0:T(2,128)(2,1)S(1)}, bf16[16,6,1,256]{3,2,1,0:T(2,128)(2,1)S(1)}, u32[]{:S(2)}, u32[]{:S(2)}) collective-permute-start(bf16[16,6,1,256]{3,2,1,0:T(2,128)(2,1)S(1)} %get-tuple-element.121), channel_id=1, source_target_pairs={{0,1},{1,2},{2,3},{4,5},{5,6},{6,7},{8,9},{9,10},{10,11},{12,13},{... | collective-permute-start | bytes 147464 | tf_op jit(solution)/shard_map/ppermute | solution.py:16
  300.2 2.2 collective-permute-start.11
  302.7 3.4 %collective-permute-done.11 = bf16[16,6,1,256]{3,2,1,0:T(2,128)(2,1)S(1)} collective-permute-done((bf16[16,6,1,256]{3,2,1,0:T(2,128)(2,1)S(1)}, bf16[16,6,1,256]{3,2,1,0:T(2,128)(2,1)S(1)}, u32[]{:S(2)}, u32[]{:S(2)}) %collective-permute-start.11) | collective-permute-done | bytes 49184 | tf_op jit(solution)/shard_map/ppermute | solution.py:19
  (352 shorter events, 59.7 us)
Async XLA Ops:
  7.2 60.4 %copy-start = (bf16[3,3,3,32,16]{3,4,2,1,0:T(8,128)(2,1)S(1)}, bf16[3,3,3,32,16]{3,4,2,1,0:T(8,128)(2,1)}, u32[]{:S(2)}) copy-start(bf16[3,3,3,32,16]{3,4,2,1,0:T(8,128)(2,1)} %param.7) | copy-start | bytes 82948
  7.2 8.9 %copy-start.2 = (bf16[16,4,8,256]{3,2,1,0:T(8,128)(2,1)S(1)}, bf16[16,4,8,256]{3,2,1,0:T(8,128)(2,1)}, u32[]{:S(2)}) copy-start(bf16[16,4,8,256]{3,2,1,0:T(8,128)(2,1)} %param.5) | copy-start | bytes 786436
  8.4 7.7 %collective-permute-start = (bf16[16,1,8,256]{3,0,2,1:T(8,128)(2,1)S(1)}, bf16[16,1,8,256]{3,0,2,1:T(8,128)(2,1)S(1)}, u32[]{:S(2)}, u32[]{:S(2)}) collective-permute-start(bf16[16,1,8,256]{3,0,2,1:T(8,128)(2,1)S(1)} %get-tuple-element.159), channel_id=1, source_target_pairs={{0,4},{4,8},{8,12},{12,16},{16,20},{20,24},{24,28},{28,32},{32,36}... | collective-permute-start | bytes 196616 | tf_op jit(solution)/shard_map/ppermute | solution.py:16
  12.7 5.2 %collective-permute-start.1 = (bf16[16,1,8,256]{3,0,2,1:T(8,128)(2,1)S(1)}, bf16[16,1,8,256]{3,0,2,1:T(8,128)(2,1)S(1)}, u32[]{:S(2)}, u32[]{:S(2)}) collective-permute-start(bf16[16,1,8,256]{3,0,2,1:T(8,128)(2,1)S(1)} %get-tuple-element.158), channel_id=1, source_target_pairs={{4,0},{8,4},{12,8},{16,12},{20,16},{24,20},{28,24},{32,28},{36,32}... | collective-permute-start | bytes 196616 | tf_op jit(solution)/shard_map/ppermute | solution.py:19
  18.0 7.1 %collective-permute-start.2 = (bf16[16,6,1,256]{3,0,2,1:T(8,128)(2,1)S(1)}, bf16[16,6,1,256]{3,0,2,1:T(8,128)(2,1)S(1)}, u32[]{:S(2)}, u32[]{:S(2)}) collective-permute-start(bf16[16,6,1,256]{3,0,2,1:T(8,128)(2,1)S(1)} %get-tuple-element.126), channel_id=1, source_target_pairs={{0,1},{1,2},{2,3},{4,5},{5,6},{6,7},{8,9},{9,10},{10,11},{12,13},{... | collective-permute-start | bytes 147464 | tf_op jit(solution)/shard_map/ppermute | solution.py:16
  23.0 5.4 %collective-permute-start.3 = (bf16[16,6,1,256]{3,0,2,1:T(8,128)(2,1)S(1)}, bf16[16,6,1,256]{3,0,2,1:T(8,128)(2,1)S(1)}, u32[]{:S(2)}, u32[]{:S(2)}) collective-permute-start(bf16[16,6,1,256]{3,0,2,1:T(8,128)(2,1)S(1)} %get-tuple-element.127), channel_id=1, source_target_pairs={{1,0},{2,1},{3,2},{5,4},{6,5},{7,6},{9,8},{10,9},{11,10},{13,12},{... | collective-permute-start | bytes 147464 | tf_op jit(solution)/shard_map/ppermute | solution.py:19
  28.7 1.0 copy-start.18
  30.1 1.0 copy-start.9
  30.1 1.1 copy-start.7
  30.1 1.2 copy-start.5
  37.0 2.5 copy-start.3
  45.3 5.3 %all-to-all-start = ((bf16[4,16,2,4,128]{4,1,3,2,0:T(8,128)(2,1)}), bf16[4,16,2,4,128]{4,1,3,2,0:T(8,128)(2,1)S(1)}, u32[]{:S(2)}, u32[]{:S(2)}) async-start(bf16[4,16,2,4,128]{4,1,3,2,0:T(8,128)(2,1)} %broadcast_in_dim.12), calls=%async_computation | async-start | bytes 262144 | tf_op jit(solution)/shard_map/all_to_all | solution.py:26
  50.7 9.4 %all-to-all-start.3 = ((bf16[32,2,4,128]{3,2,1,0:T(4,128)(2,1)}), bf16[32,2,4,128]{3,2,1,0:T(4,128)(2,1)S(1)}, u32[]{:S(2)}, u32[]{:S(2)}) async-start(bf16[32,2,4,128]{3,2,1,0:T(4,128)(2,1)} %param.9), calls=%async_computation.3 | async-start | bytes 131072 | tf_op jit(solution)/shard_map/all_to_all | solution.py:154
  55.0 74.8 %reduce-scatter.2.cloned.1.call-start = ((), (), s32[]{:S(2)}) async-start(), calls=%async_computation.5 | async-start | bytes 327680 | tf_op jit(solution)/shard_map/reduce_scatter | solution.py:158
  55.0 5.2 %collective-permute-start.4 = (bf16[16,1,16,128]{3,0,2,1:T(8,128)(2,1)S(1)}, bf16[16,1,16,128]{3,0,2,1:T(8,128)(2,1)S(1)}, u32[]{:S(2)}, u32[]{:S(2)}) collective-permute-start(bf16[16,1,16,128]{3,0,2,1:T(8,128)(2,1)S(1)} %get-tuple-element.164), channel_id=1, source_target_pairs={{0,4},{4,8},{8,12},{12,16},{16,20},{20,24},{24,28},{28,32},{32,36}... | collective-permute-start | bytes 196616 | tf_op jit(solution)/shard_map/ppermute | solution.py:16
  58.6 5.1 %collective-permute-start.5 = (bf16[16,1,16,128]{3,0,2,1:T(8,128)(2,1)S(1)}, bf16[16,1,16,128]{3,0,2,1:T(8,128)(2,1)}, u32[]{:S(2)}, u32[]{:S(2)}) collective-permute-start(bf16[16,1,16,128]{3,0,2,1:T(8,128)(2,1)S(1)} %get-tuple-element.165), channel_id=1, source_target_pairs={{4,0},{8,4},{12,8},{16,12},{20,16},{24,20},{28,24},{32,28},{36,32}... | collective-permute-start | bytes 196616 | tf_op jit(solution)/shard_map/ppermute | solution.py:19
  80.0 5.7 %collective-permute-start.6 = (bf16[8,1,16,128]{3,0,2,1:T(8,128)(2,1)S(1)}, bf16[8,1,16,128]{3,0,2,1:T(8,128)(2,1)S(1)}, u32[]{:S(2)}, u32[]{:S(2)}) collective-permute-start(bf16[8,1,16,128]{3,0,2,1:T(8,128)(2,1)S(1)} %get-tuple-element.170), channel_id=1, source_target_pairs={{0,4},{4,8},{8,12},{12,16},{16,20},{20,24},{24,28},{28,32},{32,36}... | collective-permute-start | bytes 98312 | tf_op jit(solution)/shard_map/ppermute | solution.py:16
  84.2 4.7 %collective-permute-start.7 = (bf16[8,1,16,128]{3,0,2,1:T(8,128)(2,1)S(1)}, bf16[8,1,16,128]{3,0,2,1:T(8,128)(2,1)S(1)}, u32[]{:S(2)}, u32[]{:S(2)}) collective-permute-start(bf16[8,1,16,128]{3,0,2,1:T(8,128)(2,1)S(1)} %get-tuple-element.171), channel_id=1, source_target_pairs={{4,0},{8,4},{12,8},{16,12},{20,16},{24,20},{28,24},{32,28},{36,32}... | collective-permute-start | bytes 98312 | tf_op jit(solution)/shard_map/ppermute | solution.py:19
  103.6 8.3 %all-to-all-start.2 = ((bf16[2,2,8,2,4,128]{5,2,1,4,3,0:T(8,128)(2,1)}), bf16[2,2,8,2,4,128]{5,2,1,4,3,0:T(8,128)(2,1)S(1)}, u32[]{:S(2)}, u32[]{:S(2)}) async-start(bf16[2,2,8,2,4,128]{5,2,1,4,3,0:T(8,128)(2,1)} %copy.925), calls=%async_computation.2 | async-start | bytes 131072 | tf_op jit(solution)/shard_map/all_to_all | solution.py:50
  106.9 185.9 %all-reduce.7.cloned.1.call-start = ((), (), s32[]{:S(2)}) async-start(), calls=%async_computation.6 | async-start | bytes 884736 | tf_op jit(solution)/shard_map/psum | solution.py:171
  111.9 22.8 %copy-start.17 = (f32[3,3,3,32,16]{3,4,2,1,0:T(8,128)}, f32[3,3,3,32,16]{3,4,2,1,0:T(8,128)S(1)}, u32[]{:S(2)}) copy-start(f32[3,3,3,32,16]{3,4,2,1,0:T(8,128)S(1)} %dynamic_update_slice.3) | copy-start | bytes 165892
  134.8 2.9 copy-start.4
  138.9 1.5 copy-start.14
  139.8 1.5 copy-start.12
  141.9 1.3 copy-start.10
  142.7 1.5 copy-start.8
  144.4 1.5 copy-start.6
  147.3 148.8 %collective-permute-start.8 = (bf16[16,1,8,256]{3,2,1,0:T(8,128)(2,1)S(1)}, bf16[16,1,8,256]{3,2,1,0:T(8,128)(2,1)S(1)}, u32[]{:S(2)}, u32[]{:S(2)}) collective-permute-start(bf16[16,1,8,256]{3,2,1,0:T(8,128)(2,1)S(1)} %get-tuple-element.154), channel_id=1, source_target_pairs={{0,4},{4,8},{8,12},{12,16},{16,20},{20,24},{24,28},{28,32},{32,36}... | collective-permute-start | bytes 196616 | tf_op jit(solution)/shard_map/ppermute | solution.py:16
  150.5 145.6 %collective-permute-start.9 = (bf16[16,1,8,256]{3,2,1,0:T(8,128)(2,1)S(1)}, bf16[16,1,8,256]{3,2,1,0:T(8,128)(2,1)S(1)}, u32[]{:S(2)}, u32[]{:S(2)}) collective-permute-start(bf16[16,1,8,256]{3,2,1,0:T(8,128)(2,1)S(1)} %get-tuple-element.155), channel_id=1, source_target_pairs={{4,0},{8,4},{12,8},{16,12},{20,16},{24,20},{28,24},{32,28},{36,32}... | collective-permute-start | bytes 196616 | tf_op jit(solution)/shard_map/ppermute | solution.py:19
  296.3 6.3 %collective-permute-start.10 = (bf16[16,6,1,256]{3,2,1,0:T(2,128)(2,1)S(1)}, bf16[16,6,1,256]{3,2,1,0:T(2,128)(2,1)S(1)}, u32[]{:S(2)}, u32[]{:S(2)}) collective-permute-start(bf16[16,6,1,256]{3,2,1,0:T(2,128)(2,1)S(1)} %get-tuple-element.121), channel_id=1, source_target_pairs={{0,1},{1,2},{2,3},{4,5},{5,6},{6,7},{8,9},{9,10},{10,11},{12,13},{... | collective-permute-start | bytes 147464 | tf_op jit(solution)/shard_map/ppermute | solution.py:16
  300.2 5.9 %collective-permute-start.11 = (bf16[16,6,1,256]{3,2,1,0:T(2,128)(2,1)S(1)}, bf16[16,6,1,256]{3,2,1,0:T(2,128)(2,1)S(1)}, u32[]{:S(2)}, u32[]{:S(2)}) collective-permute-start(bf16[16,6,1,256]{3,2,1,0:T(2,128)(2,1)S(1)} %get-tuple-element.122), channel_id=1, source_target_pairs={{1,0},{2,1},{3,2},{5,4},{6,5},{7,6},{9,8},{10,9},{11,10},{13,12},{... | collective-permute-start | bytes 147464 | tf_op jit(solution)/shard_map/ppermute | solution.py:19
  315.5 1.3 copy-start.1
  (6 other events, 5.1 us)
Sparse Core Ops, SparseCore 0:
  97.1 32.6 reduce-scatter.1
  147.4 145.3 all-reduce.6
where the time goes:
time: 325 us; the launch traced here: 324 us
  waiting for transfers between devices  175 us (54%)
  starting transfers between devices  44.7 us (14%)
  matrix products  41.1 us (13%)
  local copies, waits for them, and re-layouts  27.5 us (8%)
  between operations  15.8 us (5%)
  other arithmetic  13.6 us (4%)
  blocking collectives  5.82 us (2%)
    psum x1, waiting for transfers between devices, local(): fine_summed, coarse_summed = lax.psum((fine_terms, coarse_terms), GX_GY)  141 us
    dot_general x108, matrix products, correlate(): contrib = jnp.dot(matrix, piece, preferred_element_type=jnp.float32)  27.6 us
    ppermute x6, starting transfers between devices, with_halo(): lax.ppermute(lax.slice_in_dim(block, block.shape[dim] - width, None, axis...  24 us
    reduce_scatter x1, waiting for transfers between devices, local(): lax.psum_scatter(grad_terms, GY, scatter_dimension=2, tiled=True)  17.2 us
    ppermute x6, waiting for transfers between devices, with_halo(): lax.ppermute(lax.slice_in_dim(block, 0, width, axis=dim), axis, backward)  15 us
    dot_general x54, matrix products, kernel_terms(): lax.dot_general(flat_slope, piece, (((1,), (1,)), ((), ())), preferred_el...  13.5 us
    ppermute x6, starting transfers between devices, with_halo(): lax.ppermute(lax.slice_in_dim(block, 0, width, axis=dim), axis, backward)  9.45 us
    unnamed x104, local copies, waits for them, and re-layouts  6.74 us
  transfers between devices with their start and end apart: 17, of which 8 were waited for; matrix products, arithmetic and copies ran while one was open for 4% of the time, Pallas kernels for 0%

commit v1 on v0

v1 whole, which is shorter than its diff:
```python
import jax
import jax.numpy as jnp
from jax import lax
from jax.experimental import pallas as pl
from jax.experimental.pallas import tpu as pltpu
from jax.sharding import PartitionSpec as P

F32 = jnp.float32
BF16 = jnp.bfloat16
MESH = pl.DeviceIdType.MESH
C1, C2 = 16, 32
D, R, W = 4, 8, 256
HD, HR, HW = 2, 4, 128
NGX, NGY = 32, 4
DIRS = [(sx, sy) for sx in (-1, 0, 1) for sy in (-1, 0, 1) if (sx, sy) != (0, 0)]
NT = (((1,), (1,)), ((), ()))


def dot(a, b):
    return jnp.dot(a, b, preferred_element_type=F32)


def dot_nt(a, b):
    return lax.dot_general(a, b, NT, preferred_element_type=F32)


def shifted(x):
    n = x.shape[1]
    lane = lax.broadcasted_iota(jnp.int32, x.shape, 1)
    before = jnp.where(lane == 0, 0.0, pltpu.roll(x, 1, axis=1))
    after = jnp.where(lane == n - 1, 0.0, pltpu.roll(x, n - 1, axis=1))
    return before.astype(BF16), after.astype(BF16)


def exists(gx, gy, sx, sy):
    cond = None
    for ok in (
        [gx < NGX - 1] if sx == 1 else [gx > 0] if sx == -1 else []
    ) + ([gy < NGY - 1] if sy == 1 else [gy > 0] if sy == -1 else []):
        cond = ok if cond is None else jnp.logical_and(cond, ok)
    return cond


def span(s, h, n, sending):
    if s == 0:
        return h, n
    if sending:
        return (n, h) if s == 1 else (h, h)
    return (0, h) if s == 1 else (h + n, h)


class Halo:
    def __init__(self, buf, chan, h, nz, ny, send_sem, recv_sem, gx, gy):
        self.buf, self.chan, self.h, self.nz, self.ny = buf, chan, h, nz, ny
        self.send_sem, self.recv_sem, self.gx, self.gy = send_sem, recv_sem, gx, gy

    def part(self, sx, sy, sending):
        z0, zn = span(sx, self.h, self.nz, sending)
        y0, yn = span(sy, self.h, self.ny, sending)
        return self.buf.at[pl.ds(z0, zn), pl.ds(y0, yn), self.chan, :]

    def desc(self, i):
        sx, sy = DIRS[i]
        return pltpu.make_async_remote_copy(
            src_ref=self.part(sx, sy, True),
            dst_ref=self.part(sx, sy, False),
            send_sem=self.send_sem.at[i],
            recv_sem=self.recv_sem.at[i],
            device_id=(self.gx + sx, self.gy + sy),
            device_id_type=MESH,
        )

    def clear_edges(self):
        h, nz, ny = self.h, self.nz, self.ny
        for s, n, axis, g, last in (
            (-1, nz, 0, self.gx, 0),
            (1, nz, 0, self.gx, NGX - 1),
            (-1, ny, 1, self.gy, 0),
            (1, ny, 1, self.gy, NGY - 1),
        ):
            at = 0 if s == -1 else h + n
            rows = pl.ds(at, h)

            @pl.when(g == last)
            def _(axis=axis, rows=rows):
                index = (rows, slice(None)) if axis == 0 else (slice(None), rows)
                view = self.buf.at[(*index, self.chan, slice(None))]
                view[...] = jnp.zeros(view.shape, view.dtype)

    def start(self):
        for i, (sx, sy) in enumerate(DIRS):

            @pl.when(exists(self.gx, self.gy, sx, sy))
            def _(i=i):
                self.desc(i).start()

    def wait_recv(self):
        for i, (sx, sy) in enumerate(DIRS):

            @pl.when(exists(self.gx, self.gy, -sx, -sy))
            def _(i=i):
                self.desc(i).wait_recv()

    def wait_send(self):
        for i, (sx, sy) in enumerate(DIRS):

            @pl.when(exists(self.gx, self.gy, sx, sy))
            def _(i=i):
                self.desc(i).wait_send()


class AllReduce:
    def __init__(self, terms, rs, bx, fin, sems, na, nb, a, b, dev_a, dev_b):
        self.terms, self.rs, self.bx, self.fin = terms, rs, bx, fin
        self.na, self.nb, self.a, self.b = na, nb, a, b
        self.dev_a, self.dev_b = dev_a, dev_b
        self.rs_s, self.rs_r, self.b_s, self.b_r, self.g_s, self.g_r = sems

    def rs_copy(self, k):
        d = lax.rem(self.a + k, self.na)
        return pltpu.make_async_remote_copy(
            self.terms.at[d], self.rs.at[k], self.rs_s.at[k], self.rs_r.at[k], self.dev_a(d), MESH
        )

    def b_copy(self, k):
        d = lax.rem(self.b + k, self.nb)
        return pltpu.make_async_remote_copy(
            self.bx.at[self.b], self.bx.at[self.b], self.b_s.at[k], self.b_r.at[k], self.dev_b(d), MESH
        )

    def g_copy(self, k):
        d = lax.rem(self.a + k, self.na)
        return pltpu.make_async_remote_copy(
            self.fin.at[self.a], self.fin.at[self.a], self.g_s.at[k], self.g_r.at[k], self.dev_a(d), MESH
        )

    def start_scatter(self):
        for k in range(1, self.na):
            self.rs_copy(k).start()

    def start_exchange(self):
        total = self.terms[self.a]
        for k in range(1, self.na):
            self.rs_copy(k).wait_recv()
        for k in range(1, self.na):
            total = total + self.rs[k]
        self.bx[self.b] = total
        for k in range(1, self.nb):
            self.b_copy(k).start()

    def start_gather(self):
        for k in range(1, self.nb):
            self.b_copy(k).wait_recv()
        total = self.bx[0]
        for k in range(1, self.nb):
            total = total + self.bx[k]
        self.fin[self.a] = total
        for k in range(1, self.na):
            self.g_copy(k).start()

    def finish(self):
        for k in range(1, self.na):
            self.g_copy(k).wait_recv()

    def wait_send(self):
        for k in range(1, self.na):
            self.rs_copy(k).wait_send()
            self.g_copy(k).wait_send()
        for k in range(1, self.nb):
            self.b_copy(k).wait_send()


def kernel(
    vol_hbm, fcot_hbm, ccot_hbm, wf_ref, kf_ref, wc_ref, kc_ref,
    fo_ref, co_ref, vg_ref, fk_ref, ck_ref,
    raw_v, raw_f, raw_c, st_v, st_f, st_c, st_o, st_co,
    vp, cp, qp, tp, sp, fob, g1, fg, csb, wft, wct, ft, ct,
    frs, fbx, ffin, crs, cbx, cfin,
    in_sem, hs, hr, f_rs_s, f_rs_r, f_b_s, f_b_r, f_g_s, f_g_r,
    c_rs_s, c_rs_r, c_b_s, c_b_r, c_g_s, c_g_r,
):
    gx, gy = lax.axis_index("gx"), lax.axis_index("gy")
    mid = pl.ds(C1, C1)
    loads = [
        pltpu.make_async_copy(src, dst, in_sem.at[i])
        for i, (src, dst) in enumerate(
            ((vol_hbm, raw_v), (ccot_hbm, raw_c), (fcot_hbm, raw_f))
        )
    ]
    for load in loads:
        load.start()

    zi, hi = lax.rem(gx, 4), lax.div(gx, 4)
    y_lo, core = lax.div(gy, 2), lax.rem(gy, 2)
    base = hi * 4

    def c_dev_a(d):
        return (base + lax.div(d, 4), lax.rem(d, 4))

    def c_dev_b(d):
        return (d * 4 + zi, gy)

    def f_dev_a(d):
        return (base + lax.div(d, 2), lax.rem(d, 2) * 2 + core)

    def f_dev_b(d):
        return (lax.div(d, 2) * 4 + zi, y_lo * 2 + lax.rem(d, 2))

    barrier = pltpu.get_barrier_semaphore()

    def greet(device):
        pl.semaphore_signal(barrier, inc=1, device_id=device, device_id_type=MESH)

    for sx, sy in DIRS:

        @pl.when(exists(gx, gy, sx, sy))
        def _(sx=sx, sy=sy):
            greet((gx + sx, gy + sy))

    a_c, a_f, b_f = zi * 4 + gy, zi * 2 + y_lo, hi * 2 + core
    for k in range(1, 16):
        greet(c_dev_a(lax.rem(a_c + k, 16)))
        greet(f_dev_b(lax.rem(b_f + k, 16)))

    vhalo = Halo(vp, mid, 1, D, R, hs.at[0], hr.at[0], gx, gy)
    chalo = Halo(cp, slice(None), 1, HD, HR, hs.at[1], hr.at[1], gx, gy)
    qhalo = Halo(qp, mid, 2, HD, HR, hs.at[2], hr.at[2], gx, gy)
    shalo = Halo(sp, mid, 1, D, R, hs.at[3], hr.at[3], gx, gy)
    f_sum = AllReduce(
        ft, frs, fbx, ffin, (f_rs_s, f_rs_r, f_b_s, f_b_r, f_g_s, f_g_r),
        8, 16, a_f, b_f, f_dev_a, f_dev_b,
    )
    c_sum = AllReduce(
        ct, crs, cbx, cfin, (c_rs_s, c_rs_r, c_b_s, c_b_r, c_g_s, c_g_r),
        16, 8, a_c, hi, c_dev_a, c_dev_b,
    )

    eye1 = (
        lax.broadcasted_iota(jnp.int32, (C1, C1), 0) == lax.broadcasted_iota(jnp.int32, (C1, C1), 1)
    ).astype(F32).astype(BF16)
    wft[...] = dot_nt(eye1, kf_ref[...]).astype(BF16)
    wct[...] = dot_nt(eye1, kc_ref[...]).astype(BF16)
    for halo in (vhalo, chalo, qhalo, shalo):
        halo.clear_edges()

    loads[0].wait()
    for t in range(2):
        st_v[t] = raw_v[:, t * 128 : (t + 1) * 128].astype(F32)
    for z in range(D):
        for y in range(R):
            for t in range(2):
                vp[z + 1, y + 1, mid, pl.ds(t * 128, 128)] = st_v[
                    t, pl.ds(z * R + y, C1, stride=D * R), :
                ].astype(BF16)
    loads[1].wait()
    st_c[...] = raw_c[...].astype(F32)
    for z in range(HD):
        for y in range(HR):
            cp[z + 1, y + 1] = st_c[pl.ds(z * HR + y, C2, stride=HD * HR), :].astype(BF16)
    n_halo = 0
    for sx, sy in DIRS:
        n_halo = n_halo + exists(gx, gy, sx, sy).astype(jnp.int32)
    pl.semaphore_wait(barrier, n_halo + 30)
    vhalo.start()
    chalo.start()

    def put_shifts(buf, z, y, order):
        before, after = shifted(buf[z, y, mid, :].astype(F32))
        low, high = (before, after) if order > 0 else (after, before)
        buf[z, y, pl.ds(0, C1), :] = low
        buf[z, y, pl.ds(2 * C1, C1), :] = high

    def own_shifts(buf, h, nz, ny, order):
        @pl.loop(0, nz)
        def _(z):
            for y in range(ny):
                put_shifts(buf, z + h, y + h, order)

    def halo_shifts(buf, h, nz, ny, order):
        @pl.loop(0, h)
        def _(z):
            for y in range(ny + 2 * h):
                put_shifts(buf, z, y, order)
                put_shifts(buf, z + h + nz, y, order)

        @pl.loop(0, nz)
        def _(z):
            for y in range(h):
                put_shifts(buf, z + h, y, order)
                put_shifts(buf, z + h, y + h + ny, order)

    def taps(buf, z, y, back=False):
        rows = []
        for a in range(3):
            for b in range(3):
                da, db = (2 - a, 2 - b) if back else (a, b)
                rows.append(buf[z + da, y + db])
        return jnp.concatenate(rows, axis=0)

    own_shifts(vp, 1, D, R, 1)
    loads[2].wait()
    for t in range(2):
        st_f[t] = raw_f[:, t * 128 : (t + 1) * 128].astype(F32)
    pool_row = lax.broadcasted_iota(jnp.int32, (W, HW), 0)
    pool_col = lax.broadcasted_iota(jnp.int32, (W, HW), 1)
    pool_mat = (lax.div(pool_row, 2) == pool_col).astype(F32).astype(BF16)
    vhalo.wait_recv()
    halo_shifts(vp, 1, D, R, 1)
    wf = wf_ref[...]

    @pl.loop(0, HD)
    def _(zc):
        for zz in range(2):
            z = zc * 2 + zz
            for y in range(R):
                pre = dot(wf, taps(vp, z, y))
                s = jax.nn.sigmoid(pre)
                out = (vp[z + 1, y + 1, mid, :].astype(F32) + pre * s).astype(BF16)
                g1[z, y] = s * (1.0 + pre * (1.0 - s))
                fob[z, y] = out
                out = out.astype(F32)
                for t in range(2):
                    st_o[t, pl.ds(z * R + y, C1, stride=D * R), :] = out[:, t * 128 : (t + 1) * 128]
        for yc in range(HR):
            four = fob[pl.ds(zc * 2, 2), pl.ds(yc * 2, 2)].reshape(4 * C1, W)
            half = dot(four, pool_mat)
            total = half[0:16] + half[16:32] + half[32:48] + half[48:64]
            qp[zc + 2, yc + 2, mid, :] = (total * 0.125).astype(BF16)

    qhalo.start()
    for t in range(2):
        fo_ref[:, t * 128 : (t + 1) * 128] = st_o[t].astype(BF16)
    own_shifts(qp, 2, HD, HR, 1)
    up_row = lax.broadcasted_iota(jnp.int32, (HW, 3 * W), 0)
    up_col = lax.broadcasted_iota(jnp.int32, (HW, 3 * W), 1)
    up_mat = (
        up_row == lax.div(lax.rem(up_col, W), 2) + 1 - lax.div(up_col, W)
    ).astype(F32).astype(BF16)
    wc = wc_ref[...]
    chalo.wait_recv()
    qhalo.wait_recv()
    halo_shifts(qp, 2, HD, HR, 1)

    @pl.loop(0, HD + 2)
    def _(z):
        for y in range(HR + 2):
            pre = dot(wc, taps(qp, z, y))
            s = jax.nn.sigmoid(pre)
            slope = cp[z, y].astype(F32) * (s * (1.0 + pre * (1.0 - s)))
            csb[z, y] = slope.astype(BF16)
            if 1 <= y <= HR:

                @pl.when(jnp.logical_and(z >= 1, z <= HD))
                def _(y=y, pre=pre, s=s):
                    st_co[pl.ds((z - 1) * HR + y - 1, C2, stride=HD * HR), :] = (
                        (pre * s).astype(BF16).astype(F32)
                    )
        wide = dot(csb[z].reshape((HR + 2) * C2, HW), up_mat).astype(BF16)
        for c in range(3):
            tp[z, :, pl.ds(c * C2, C2), :] = wide[:, c * W : (c + 1) * W].reshape(HR + 2, C2, W)

    co_ref[...] = st_co[...].astype(BF16)

    ck = jnp.zeros((C2, 27 * C1), F32)
    for z in range(HD):
        for y in range(HR):
            ck = ck + dot_nt(csb[z + 1, y + 1], taps(qp, z + 1, y + 1))
    ck = jnp.concatenate([ck, jnp.zeros((C2, 80), F32)], axis=1)
    for i in range(4):
        for t in range(4):
            ct[i * 4 + t] = ck[i * 8 : (i + 1) * 8, t * 128 : (t + 1) * 128]
    c_sum.start_scatter()

    wct_v = wct[...]

    @pl.loop(0, HD)
    def _(zc):
        for yc in range(HR):
            spread = dot(wct_v, taps(tp, zc, yc, True)) * 0.125
            for zz in range(2):
                for yy in range(2):
                    z, y = zc * 2 + zz, yc * 2 + yy
                    cot = jnp.concatenate(
                        [st_f[t, pl.ds(z * R + y, C1, stride=D * R), :] for t in range(2)], axis=1
                    )
                    grad = cot + spread
                    fg[z, y] = grad
                    sp[z + 1, y + 1, mid, :] = (grad * g1[z, y]).astype(BF16)

    shalo.start()
    c_sum.start_exchange()

    def fine_terms(z, acc):
        for y in range(R):
            acc = acc + dot_nt(sp[z + 1, y + 1, mid, :], taps(vp, z, y))
        return acc

    fk = lax.fori_loop(0, D, fine_terms, jnp.zeros((C1, 27 * C1), F32))
    fk = jnp.concatenate([fk, jnp.zeros((C1, 80), F32)], axis=1)
    for i in range(2):
        for t in range(4):
            ft[i * 4 + t] = fk[i * 8 : (i + 1) * 8, t * 128 : (t + 1) * 128]
    f_sum.start_scatter()
    c_sum.start_gather()
    own_shifts(sp, 1, D, R, -1)
    f_sum.start_exchange()
    shalo.wait_recv()
    halo_shifts(sp, 1, D, R, -1)
    wft_v = wft[...]

    def volume_rows(z):
        for y in range(R):
            total = fg[z, y] + dot(wft_v, taps(sp, z, y, True))
            for t in range(2):
                st_o[t, pl.ds(z * R + y, C1, stride=D * R), :] = total[:, t * 128 : (t + 1) * 128]

    @pl.loop(0, HD)
    def _(z):
        volume_rows(z)

    f_sum.start_gather()

    @pl.loop(HD, D)
    def _(z):
        volume_rows(z)

    for t in range(2):
        vg_ref[:, t * 128 : (t + 1) * 128] = st_o[t].astype(BF16)

    def emit(fin, out, rows, scale):
        for i in range(rows):
            for t in range(4):
                tile = fin[i * 4 + t] * scale
                for k in range(8):
                    tap = t * 8 + k
                    if tap < 27:
                        out[tap, pl.ds(i * 8, 8), :] = tile[:, k * C1 : (k + 1) * C1]

    c_sum.finish()
    emit(cfin, ck_ref, 4, 131072.0**-0.5)
    f_sum.finish()
    emit(ffin, fk_ref, 2, 1048576.0**-0.5)
    for one in (vhalo, chalo, qhalo, shalo, c_sum, f_sum):
        one.wait_send()


def local(volume, fine_kernel, coarse_kernel, fine_cotangent, coarse_cotangent):
    wf = fine_kernel.transpose(3, 0, 1, 2, 4).reshape(C1, 27 * C1)
    wc = coarse_kernel.transpose(3, 0, 1, 2, 4).reshape(C2, 27 * C1)
    kf = fine_kernel.reshape(27 * C1, C1)
    kc = coarse_kernel.reshape(27 * C2, C1)
    any_spec = pl.BlockSpec(memory_space=pl.ANY)
    vmem = pl.BlockSpec(memory_space=pltpu.VMEM)
    dma = pltpu.SemaphoreType.DMA
    V = pltpu.VMEM
    tile = (8, 128)
    outs = pl.pallas_call(
        kernel,
        out_shape=[
            jax.ShapeDtypeStruct((C1 * D * R, W), BF16),
            jax.ShapeDtypeStruct((C2 * HD * HR, HW), BF16),
            jax.ShapeDtypeStruct((C1 * D * R, W), BF16),
            jax.ShapeDtypeStruct((27, C1, C1), F32),
            jax.ShapeDtypeStruct((27, C2, C1), F32),
        ],
        in_specs=[any_spec] * 3 + [vmem] * 4,
        out_specs=[vmem] * 5,
        scratch_shapes=[
            V((C1 * D * R, W), BF16), V((C1 * D * R, W), BF16), V((C2 * HD * HR, HW), BF16),
            V((2, C1 * D * R, 128), F32), V((2, C1 * D * R, 128), F32), V((C2 * HD * HR, HW), F32),
            V((2, C1 * D * R, 128), F32), V((C2 * HD * HR, HW), F32),
            V((D + 2, R + 2, 3 * C1, W), BF16),
            V((HD + 2, HR + 2, C2, HW), BF16),
            V((HD + 4, HR + 4, 3 * C1, HW), BF16),
            V((HD + 2, HR + 2, 3 * C2, W), BF16),
            V((D + 2, R + 2, 3 * C1, W), BF16),
            V((D, R, C1, W), BF16), V((D, R, C1, W), F32), V((D, R, C1, W), F32),
            V((HD + 2, HR + 2, C2, HW), BF16),
            V((C1, 27 * C1), BF16), V((C1, 27 * C2), BF16),
            V((8, *tile), F32), V((16, *tile), F32),
            V((8, *tile), F32), V((16, *tile), F32), V((8, *tile), F32),
            V((16, *tile), F32), V((8, *tile), F32), V((16, *tile), F32),
            dma((3,)), dma((4, 8)), dma((4, 8)),
            dma((8,)), dma((8,)), dma((16,)), dma((16,)), dma((8,)), dma((8,)),
            dma((16,)), dma((16,)), dma((8,)), dma((8,)), dma((16,)), dma((16,)),
        ],
        compiler_params=pltpu.CompilerParams(
            collective_id=0, has_side_effects=True, vmem_limit_bytes=48 << 20
        ),
        name="unet_levels",
    )(
        volume.reshape(C1 * D * R, W),
        fine_cotangent.reshape(C1 * D * R, W),
        coarse_cotangent.reshape(C2 * HD * HR, HW),
        wf, kf, wc, kc,
    )
    fo, co, vg, fk, ck = outs
    return (
        fo.reshape(volume.shape),
        co.reshape(coarse_cotangent.shape),
        vg.reshape(volume.shape),
        fk.reshape(fine_kernel.shape),
        ck.reshape(coarse_kernel.shape),
    )


def solution(mesh):
    block = P(None, "gx", "gy", None)
    return jax.shard_map(
        local,
        mesh=mesh,
        in_specs=(block, P(), P(), block, block),
        out_specs=(block, block, block, P(), P()),
        check_vma=False,
    )
```

time: 325 us -> 54.7 us (0.17)
  waiting for transfers between devices: 175 us -> 0 us
  Pallas kernels: 0 us -> 47.4 us
  starting transfers between devices: 44.7 us -> 0 us
  matrix products: 41.1 us -> 0 us
  local copies, waits for them, and re-layouts: 27.5 us -> 6.32 us
  between operations: 15.8 us -> 0.72 us
  other arithmetic: 13.6 us -> 0 us
  blocking collectives: 5.82 us -> 0 us
    psum x1 -> x0, waiting for transfers between devices: 141 us -> none  [local(): fine_summed, coarse_summed = lax.psum((fine_terms, coarse_terms), GX_GY)]
    pallas_call x0 -> x1, Pallas kernels: none -> 47.4 us  [local(): pl.pallas_call(kernel, out_shape=[jax.ShapeDtypeStruct((C1 * D * R, W), B...]
    dot_general x162 -> x0, matrix products: 41.1 us -> none  [the longest x108 27.6 us: correlate(): contrib = jnp.dot(matrix, piece, preferred_element_type=jnp.float32)]
    ppermute x12 -> x0, starting transfers between devices: 33.5 us -> none  [the longest x6 24 us: with_halo(): lax.ppermute(lax.slice_in_dim(block, block.shape[dim] - width, None, axis...]
    reduce_scatter x1 -> x0, waiting for transfers between devices: 17.2 us -> none  [local(): lax.psum_scatter(grad_terms, GY, scatter_dimension=2, tiled=True)]
    ppermute x12 -> x0, waiting for transfers between devices: 15.1 us -> none  [the longest x6 15 us: with_halo(): lax.ppermute(lax.slice_in_dim(block, 0, width, axis=dim), axis, backward)]
    all_to_all x3 -> x0, starting transfers between devices: 10.9 us -> none  [the longest x1 4.29 us: local(): lax.all_to_all(coarse_cotangent, GY, split_axis=0, concat_axis=2, tiled=T...]
    all_to_all x1 -> x0, blocking collectives: 5.82 us -> none  [moved_by_axis(): whole = lax.all_to_all(whole, axes[k], k, k, tiled=True)]
  transfers between devices with their start and end apart: 17 -> 0, of which waited for: 8 -> 0; matrix products, arithmetic and copies ran while one was open for 4% -> 0% of each run, Pallas kernels for 0% -> 0%
where the time goes in v1:
time: 54.7 us; the launch traced here: 54.5 us
  Pallas kernels  47.4 us (87%)
  local copies, waits for them, and re-layouts  6.32 us (12%)
  between operations  0.72 us (1%)
    pallas_call x1, Pallas kernels, local(): pl.pallas_call(kernel, out_shape=[jax.ShapeDtypeStruct((C1 * D * R, W), B...  47.4 us
    unnamed x16, local copies, waits for them, and re-layouts  5.13 us

profile of v1, /device:TPU:1, one launch (start us, length us, event | category | flops | bytes accessed | tf_op | source)
XLA Modules:
  0.0 54.5 jit_solution(12021504594713449593)
XLA Ops:
  0.6 0.0 copy-start
  0.6 1.0 %copy.16.wc_ref = bf16[32,432]{1,0:T(8,128)(2,1)S(1)} copy(bf16[32,432]{0,1:T(8,128)(2,1)} %bitcast.25) | data formatting | bytes 55296 | tf_op jit(solution)/shard_map/reshape | solution.py:449
  1.7 0.0 copy-done
  1.7 0.0 copy-start.4
  1.7 0.0 copy-start.2
  1.7 0.1 copy.14
  1.8 0.0 copy-start.1
  1.8 0.1 reshape.49.wf_ref
  1.9 0.7 %copy-done.4 = bf16[3,3,3,32,16]{3,4,2,1,0:T(8,128)(2,1)S(1)} copy-done((bf16[3,3,3,32,16]{3,4,2,1,0:T(8,128)(2,1)S(1)}, bf16[3,3,3,32,16]{3,4,2,1,0:T(8,128)(2,1)}, u32[]{:S(2)}) %copy-start.4) | copy-done | bytes 27672
  2.6 0.0 copy-start.3
  2.6 0.2 copy.15
  2.7 0.0 copy-done.2
  2.7 0.0 copy-done.1
  2.8 0.7 %copy-done.3 = bf16[32,2,4,128]{3,2,1,0:T(4,128)(2,1)S(1)} copy-done((bf16[32,2,4,128]{3,2,1,0:T(4,128)(2,1)S(1)}, bf16[32,2,4,128]{3,2,1,0:T(4,128)(2,1)}, u32[]{:S(2)}) %copy-start.3) | copy-done | bytes 65560
  3.4 47.4 %unet_levels.1 = (bf16[512,256]{1,0:T(8,128)(2,1)S(1)}, bf16[256,128]{1,0:T(8,128)(2,1)S(1)}, bf16[512,256]{1,0:T(8,128)(2,1)S(1)}, f32[27,16,16]{2,1,0:T(8,128)S(1)}, f32[27,32,16]{2,1,0:T(8,128)S(1)}) custom-call(bf16[512,256]{1,0:T(8,128)(2,1)S(1)} %bitcast.20, bf16[512,256]{1,0:T(8,128)(2,1)S(1)} %bitcast.21, bf16[256,128]{1,0:T(8,128)(2,1)S(1)} %bitcast.24, ...), custom_call_target="tpu_custom_call" | custom-call | tf_op jit(solution)/shard_map/unet_levels/pallas_call | solution.py:457
  50.9 0.9 %copy.17 = f32[3,3,3,32,16]{3,4,2,1,0:T(8,128)} copy(f32[3,3,3,32,16]{4,3,2,1,0:T(8,128)S(1)} %bitcast.15) | data formatting | bytes 110592
  51.8 0.7 %copy.22 = bf16[16,4,8,256]{3,2,1,0:T(8,128)(2,1)} copy(bf16[16,4,8,256]{3,2,1,0:T(8,128)(2,1)S(1)} %bitcast.19) | data formatting | bytes 524288
  52.5 0.6 %copy.23 = bf16[32,2,4,128]{3,2,1,0:T(4,128)(2,1)} copy(bf16[32,2,4,128]{3,2,1,0:T(4,128)(2,1)S(1)} %bitcast.23) | data formatting | bytes 131072
  53.1 0.7 %copy.24 = bf16[16,4,8,256]{3,2,1,0:T(8,128)(2,1)} copy(bf16[16,4,8,256]{3,2,1,0:T(8,128)(2,1)S(1)} %bitcast.18) | data formatting | bytes 524288
  53.8 0.7 %copy.25 = f32[3,3,3,16,16]{4,3,2,1,0:T(8,128)} copy(f32[3,3,3,16,16]{4,3,2,1,0:T(8,128)S(1)} %bitcast.22) | data formatting | bytes 55296
Async XLA Ops:
  0.6 1.0 %copy-start = (bf16[3,3,3,16,16]{4,3,2,1,0:T(8,128)(2,1)S(1)}, bf16[3,3,3,16,16]{4,3,2,1,0:T(8,128)(2,1)}, u32[]{:S(2)}) copy-start(bf16[3,3,3,16,16]{4,3,2,1,0:T(8,128)(2,1)} %param.6) | copy-start | bytes 41476
  1.7 0.9 %copy-start.4 = (bf16[3,3,3,32,16]{3,4,2,1,0:T(8,128)(2,1)S(1)}, bf16[3,3,3,32,16]{3,4,2,1,0:T(8,128)(2,1)}, u32[]{:S(2)}) copy-start(bf16[3,3,3,32,16]{3,4,2,1,0:T(8,128)(2,1)} %param.7) | copy-start | bytes 82948
  1.7 1.1 %copy-start.2 = (bf16[16,4,8,256]{3,2,1,0:T(8,128)(2,1)S(1)}, bf16[16,4,8,256]{3,2,1,0:T(8,128)(2,1)}, u32[]{:S(2)}) copy-start(bf16[16,4,8,256]{3,2,1,0:T(8,128)(2,1)} %param.8) | copy-start | bytes 786436
  1.8 1.0 %copy-start.1 = (bf16[16,4,8,256]{3,2,1,0:T(8,128)(2,1)S(1)}, bf16[16,4,8,256]{3,2,1,0:T(8,128)(2,1)}, u32[]{:S(2)}) copy-start(bf16[16,4,8,256]{3,2,1,0:T(8,128)(2,1)} %param.5) | copy-start | bytes 786436
  2.6 0.9 %copy-start.3 = (bf16[32,2,4,128]{3,2,1,0:T(4,128)(2,1)S(1)}, bf16[32,2,4,128]{3,2,1,0:T(4,128)(2,1)}, u32[]{:S(2)}) copy-start(bf16[32,2,4,128]{3,2,1,0:T(4,128)(2,1)} %param.9) | copy-start | bytes 196612

commit v2 on v1

--- a/solution.py
+++ b/solution.py
@@ -171,20 +171,35 @@
 
 
 def kernel(
-    vol_hbm, fcot_hbm, ccot_hbm, wf_ref, kf_ref, wc_ref, kc_ref,
-    fo_ref, co_ref, vg_ref, fk_ref, ck_ref,
-    raw_v, raw_f, raw_c, st_v, st_f, st_c, st_o, st_co,
-    vp, cp, qp, tp, sp, fob, g1, fg, csb, wft, wct, ft, ct,
-    frs, fbx, ffin, crs, cbx, cfin,
-    in_sem, hs, hr, f_rs_s, f_rs_r, f_b_s, f_b_r, f_g_s, f_g_r,
+    vol_hbm, fcot_hbm, ccot_hbm, kf_hbm, kc_hbm,
+    fo_ref, co_ref, vg_ref, ffin, cfin,
+    raw_v, raw_f, raw_c, kf, kc, st_v, st_f, st_c, st_o, st_co,
+    vp, cp, qp, tp, sp, fob, g1, fg, csb, cob, w32, wc32, wft, ft, ct,
+    frs, fbx, crs, cbx,
+    in_sem, hs, hr, know, f_rs_s, f_rs_r, f_b_s, f_b_r, f_g_s, f_g_r,
     c_rs_s, c_rs_r, c_b_s, c_b_r, c_g_s, c_g_r,
 ):
     gx, gy = lax.axis_index("gx"), lax.axis_index("gy")
     mid = pl.ds(C1, C1)
+    barrier = pltpu.get_barrier_semaphore()
+    n_halo = 0
+    for sx, sy in DIRS:
+        near = exists(gx, gy, sx, sy)
+        n_halo = n_halo + near.astype(jnp.int32)
+
+        @pl.when(near)
+        def _(sx=sx, sy=sy):
+            pl.semaphore_signal(
+                barrier, inc=1, device_id=(gx + sx, gy + sy), device_id_type=MESH
+            )
+
     loads = [
         pltpu.make_async_copy(src, dst, in_sem.at[i])
         for i, (src, dst) in enumerate(
-            ((vol_hbm, raw_v), (ccot_hbm, raw_c), (fcot_hbm, raw_f))
+            (
+                (vol_hbm, raw_v), (kf_hbm, kf), (kc_hbm, kc),
+                (ccot_hbm, raw_c), (fcot_hbm, raw_f),
+            )
         )
     ]
     for load in loads:
@@ -201,26 +216,31 @@
         return (d * 4 + zi, gy)
 
     def f_dev_a(d):
-        return (base + lax.div(d, 2), lax.rem(d, 2) * 2 + core)
+        return (base + lax.div(d, 2), y_lo * 2 + lax.rem(d, 2))
 
     def f_dev_b(d):
-        return (lax.div(d, 2) * 4 + zi, y_lo * 2 + lax.rem(d, 2))
-
-    barrier = pltpu.get_barrier_semaphore()
-
-    def greet(device):
-        pl.semaphore_signal(barrier, inc=1, device_id=device, device_id_type=MESH)
-
-    for sx, sy in DIRS:
-
-        @pl.when(exists(gx, gy, sx, sy))
-        def _(sx=sx, sy=sy):
-            greet((gx + sx, gy + sy))
-
-    a_c, a_f, b_f = zi * 4 + gy, zi * 2 + y_lo, hi * 2 + core
-    for k in range(1, 16):
-        greet(c_dev_a(lax.rem(a_c + k, 16)))
-        greet(f_dev_b(lax.rem(b_f + k, 16)))
+        return (lax.div(d, 2) * 4 + zi, lax.rem(d, 2) * 2 + core)
+
+    a_c, a_f, b_f = zi * 4 + gy, zi * 2 + core, hi * 2 + y_lo
+
+    def spread_word(step):
+        reach = 2 << step
+        for side, sign in enumerate((1, -1)):
+
+            @pl.when((gx < NGX - reach) if sign == 1 else (gx >= reach))
+            def _(side=side, sign=sign):
+                pl.semaphore_signal(
+                    know.at[step, side], inc=1,
+                    device_id=(gx + sign * reach, gy), device_id_type=MESH,
+                )
+
+    def hear_word(step):
+        reach = 2 << step
+        for side, sign in enumerate((1, -1)):
+
+            @pl.when((gx >= reach) if sign == 1 else (gx < NGX - reach))
+            def _(side=side):
+                pl.semaphore_wait(know.at[step, side], 1)
 
     vhalo = Halo(vp, mid, 1, D, R, hs.at[0], hr.at[0], gx, gy)
     chalo = Halo(cp, slice(None), 1, HD, HR, hs.at[1], hr.at[1], gx, gy)
@@ -234,12 +254,6 @@
         ct, crs, cbx, cfin, (c_rs_s, c_rs_r, c_b_s, c_b_r, c_g_s, c_g_r),
         16, 8, a_c, hi, c_dev_a, c_dev_b,
     )
-
-    eye1 = (
-        lax.broadcasted_iota(jnp.int32, (C1, C1), 0) == lax.broadcasted_iota(jnp.int32, (C1, C1), 1)
-    ).astype(F32).astype(BF16)
-    wft[...] = dot_nt(eye1, kf_ref[...]).astype(BF16)
-    wct[...] = dot_nt(eye1, kc_ref[...]).astype(BF16)
     for halo in (vhalo, chalo, qhalo, shalo):
         halo.clear_edges()
 
@@ -252,17 +266,8 @@
                 vp[z + 1, y + 1, mid, pl.ds(t * 128, 128)] = st_v[
                     t, pl.ds(z * R + y, C1, stride=D * R), :
                 ].astype(BF16)
-    loads[1].wait()
-    st_c[...] = raw_c[...].astype(F32)
-    for z in range(HD):
-        for y in range(HR):
-            cp[z + 1, y + 1] = st_c[pl.ds(z * HR + y, C2, stride=HD * HR), :].astype(BF16)
-    n_halo = 0
-    for sx, sy in DIRS:
-        n_halo = n_halo + exists(gx, gy, sx, sy).astype(jnp.int32)
-    pl.semaphore_wait(barrier, n_halo + 30)
+    pl.semaphore_wait(barrier, n_halo)
     vhalo.start()
-    chalo.start()
 
     def put_shifts(buf, z, y, order):
         before, after = shifted(buf[z, y, mid, :].astype(F32))
@@ -298,29 +303,63 @@
         return jnp.concatenate(rows, axis=0)
 
     own_shifts(vp, 1, D, R, 1)
-    loads[2].wait()
-    for t in range(2):
-        st_f[t] = raw_f[:, t * 128 : (t + 1) * 128].astype(F32)
+    for one in (1, 2):
+        loads[one].wait()
+    for tap in range(27):
+        w32[:, tap * C1 : (tap + 1) * C1] = kf[tap * C1 : (tap + 1) * C1, :].astype(F32)
+        wc32[:, tap * C2 : (tap + 1) * C2] = kc[tap * C1 : (tap + 1) * C1, :].astype(F32)
+
+    def eye(n):
+        rows = lax.broadcasted_iota(jnp.int32, (n, n), 0)
+        return (rows == lax.broadcasted_iota(jnp.int32, (n, n), 1)).astype(F32).astype(BF16)
+
+    wf = w32[...].astype(BF16)
+    wft[...] = dot_nt(eye(C1), kf[...]).astype(BF16)
+    loads[3].wait()
+    st_c[...] = raw_c[...].astype(F32)
+    for z in range(HD):
+        for y in range(HR):
+            cp[z + 1, y + 1] = st_c[pl.ds(z * HR + y, C2, stride=HD * HR), :].astype(BF16)
+    chalo.start()
+
+    def fine_row(z, y):
+        pre = dot(wf, taps(vp, z, y))
+        s = jax.nn.sigmoid(pre)
+        out = (vp[z + 1, y + 1, mid, :].astype(F32) + pre * s).astype(BF16)
+        g1[z, y] = s * (1.0 + pre * (1.0 - s))
+        fob[z, y] = out
+
+    @pl.loop(1, D - 1)
+    def _(z):
+        for y in range(1, R - 1):
+            fine_row(z, y)
+
+    wc = dot_nt(eye(C2), kc[...]).astype(BF16)
+    wct = wc32[...].astype(BF16)
     pool_row = lax.broadcasted_iota(jnp.int32, (W, HW), 0)
     pool_col = lax.broadcasted_iota(jnp.int32, (W, HW), 1)
     pool_mat = (lax.div(pool_row, 2) == pool_col).astype(F32).astype(BF16)
+    up_row = lax.broadcasted_iota(jnp.int32, (HW, 3 * W), 0)
+    up_col = lax.broadcasted_iota(jnp.int32, (HW, 3 * W), 1)
+    up_mat = (
+        up_row == lax.div(lax.rem(up_col, W), 2) + 1 - lax.div(up_col, W)
+    ).astype(F32).astype(BF16)
+    loads[4].wait()
+    for t in range(2):
+        st_f[t] = raw_f[:, t * 128 : (t + 1) * 128].astype(F32)
     vhalo.wait_recv()
+    spread_word(0)
     halo_shifts(vp, 1, D, R, 1)
-    wf = wf_ref[...]
+
+    @pl.loop(0, 2)
+    def _(side):
+        for y in range(R):
+            fine_row(side * (D - 1), y)
+        for y in (0, R - 1):
+            fine_row(side + 1, y)
 
     @pl.loop(0, HD)
     def _(zc):
-        for zz in range(2):
-            z = zc * 2 + zz
-            for y in range(R):
-                pre = dot(wf, taps(vp, z, y))
-                s = jax.nn.sigmoid(pre)
-                out = (vp[z + 1, y + 1, mid, :].astype(F32) + pre * s).astype(BF16)
-                g1[z, y] = s * (1.0 + pre * (1.0 - s))
-                fob[z, y] = out
-                out = out.astype(F32)
-                for t in range(2):
-                    st_o[t, pl.ds(z * R + y, C1, stride=D * R), :] = out[:, t * 128 : (t + 1) * 128]
         for yc in range(HR):
             four = fob[pl.ds(zc * 2, 2), pl.ds(yc * 2, 2)].reshape(4 * C1, W)
             half = dot(four, pool_mat)
@@ -328,15 +367,23 @@
             qp[zc + 2, yc + 2, mid, :] = (total * 0.125).astype(BF16)
 
     qhalo.start()
+    own_shifts(qp, 2, HD, HR, 1)
+    hear_word(0)
+    spread_word(1)
+
+    def rows_out(rows, store):
+        @pl.loop(0, D)
+        def _(z):
+            for y in range(R):
+                value = rows[z, y].astype(F32)
+                for t in range(2):
+                    store[t, pl.ds(z * R + y, C1, stride=D * R), :] = value[
+                        :, t * 128 : (t + 1) * 128
+                    ]
+
+    rows_out(fob, st_o)
     for t in range(2):
         fo_ref[:, t * 128 : (t + 1) * 128] = st_o[t].astype(BF16)
-    own_shifts(qp, 2, HD, HR, 1)
-    up_row = lax.broadcasted_iota(jnp.int32, (HW, 3 * W), 0)
-    up_col = lax.broadcasted_iota(jnp.int32, (HW, 3 * W), 1)
-    up_mat = (
-        up_row == lax.div(lax.rem(up_col, W), 2) + 1 - lax.div(up_col, W)
-    ).astype(F32).astype(BF16)
-    wc = wc_ref[...]
     chalo.wait_recv()
     qhalo.wait_recv()
     halo_shifts(qp, 2, HD, HR, 1)
@@ -349,18 +396,13 @@
             slope = cp[z, y].astype(F32) * (s * (1.0 + pre * (1.0 - s)))
             csb[z, y] = slope.astype(BF16)
             if 1 <= y <= HR:
-
-                @pl.when(jnp.logical_and(z >= 1, z <= HD))
-                def _(y=y, pre=pre, s=s):
-                    st_co[pl.ds((z - 1) * HR + y - 1, C2, stride=HD * HR), :] = (
-                        (pre * s).astype(BF16).astype(F32)
-                    )
+                cob[z, y - 1] = (pre * s).astype(BF16)
         wide = dot(csb[z].reshape((HR + 2) * C2, HW), up_mat).astype(BF16)
         for c in range(3):
             tp[z, :, pl.ds(c * C2, C2), :] = wide[:, c * W : (c + 1) * W].reshape(HR + 2, C2, W)
 
-    co_ref[...] = st_co[...].astype(BF16)
-
+    hear_word(1)
+    spread_word(2)
     ck = jnp.zeros((C2, 27 * C1), F32)
     for z in range(HD):
         for y in range(HR):
@@ -371,12 +413,10 @@
             ct[i * 4 + t] = ck[i * 8 : (i + 1) * 8, t * 128 : (t + 1) * 128]
     c_sum.start_scatter()
 
-    wct_v = wct[...]
-
     @pl.loop(0, HD)
     def _(zc):
         for yc in range(HR):
-            spread = dot(wct_v, taps(tp, zc, yc, True)) * 0.125
+            spread = dot(wct, taps(tp, zc, yc, True)) * 0.125
             for zz in range(2):
                 for yy in range(2):
                     z, y = zc * 2 + zz, yc * 2 + yy
@@ -388,7 +428,8 @@
                     sp[z + 1, y + 1, mid, :] = (grad * g1[z, y]).astype(BF16)
 
     shalo.start()
-    c_sum.start_exchange()
+    hear_word(2)
+    spread_word(3)
 
     def fine_terms(z, acc):
         for y in range(R):
@@ -401,86 +442,102 @@
         for t in range(4):
             ft[i * 4 + t] = fk[i * 8 : (i + 1) * 8, t * 128 : (t + 1) * 128]
     f_sum.start_scatter()
-    c_sum.start_gather()
+    hear_word(3)
+    c_sum.start_exchange()
     own_shifts(sp, 1, D, R, -1)
     f_sum.start_exchange()
     shalo.wait_recv()
     halo_shifts(sp, 1, D, R, -1)
     wft_v = wft[...]
 
-    def volume_rows(z):
+    @pl.loop(0, D)
+    def _(z):
         for y in range(R):
-            total = fg[z, y] + dot(wft_v, taps(sp, z, y, True))
-            for t in range(2):
-                st_o[t, pl.ds(z * R + y, C1, stride=D * R), :] = total[:, t * 128 : (t + 1) * 128]
-
-    @pl.loop(0, HD)
-    def _(z):
-        volume_rows(z)
-
+            fg[z, y] = fg[z, y] + dot(wft_v, taps(sp, z, y, True))
+
+    c_sum.start_gather()
     f_sum.start_gather()
-
-    @pl.loop(HD, D)
-    def _(z):
-        volume_rows(z)
-
+    rows_out(fg, st_o)
     for t in range(2):
         vg_ref[:, t * 128 : (t + 1) * 128] = st_o[t].astype(BF16)
-
-    def emit(fin, out, rows, scale):
-        for i in range(rows):
-            for t in range(4):
-                tile = fin[i * 4 + t] * scale
-                for k in range(8):
-                    tap = t * 8 + k
-                    if tap < 27:
-                        out[tap, pl.ds(i * 8, 8), :] = tile[:, k * C1 : (k + 1) * C1]
-
+    for z in range(HD):
+        for y in range(HR):
+            st_co[pl.ds(z * HR + y, C2, stride=HD * HR), :] = cob[z + 1, y].astype(F32)
+    co_ref[...] = st_co[...].astype(BF16)
+    for one in (vhalo, chalo, qhalo, shalo):
+        one.wait_send()
     c_sum.finish()
-    emit(cfin, ck_ref, 4, 131072.0**-0.5)
     f_sum.finish()
-    emit(ffin, fk_ref, 2, 1048576.0**-0.5)
-    for one in (vhalo, chalo, qhalo, shalo, c_sum, f_sum):
+    for one in (c_sum, f_sum):
         one.wait_send()
 
 
+def emit_kernel(fo, co, vg, ffin, cfin, fo_hbm, co_hbm, vg_hbm, fk_hbm, ck_hbm, fk, ck, sem):
+    copies = [
+        pltpu.make_async_copy(src, dst, sem.at[i])
+        for i, (src, dst) in enumerate(
+            ((fo, fo_hbm), (vg, vg_hbm), (co, co_hbm), (fk, fk_hbm), (ck, ck_hbm))
+        )
+    ]
+    for i in range(3):
+        copies[i].start()
+    for i in range(2):
+        for t in range(4):
+            tile = ffin[i * 4 + t] * (1048576.0**-0.5)
+            for k in range(8):
+                tap = t * 8 + k
+                if tap < 27:
+                    fk[tap, pl.ds(i * 8, 8), :] = tile[:, k * C1 : (k + 1) * C1]
+    copies[3].start()
+    for t in range(4):
+        rows = jnp.concatenate([cfin[i * 4 + t] for i in range(4)], axis=0)
+        cols = jnp.transpose(rows * (131072.0**-0.5))
+        for k in range(8):
+            tap = t * 8 + k
+            if tap < 27:
+                ck[tap] = cols[k * C1 : (k + 1) * C1, :]
+    copies[4].start()
+    for one in copies:
+        one.wait()
+
+
 def local(volume, fine_kernel, coarse_kernel, fine_cotangent, coarse_cotangent):
-    wf = fine_kernel.transpose(3, 0, 1, 2, 4).reshape(C1, 27 * C1)
-    wc = coarse_kernel.transpose(3, 0, 1, 2, 4).reshape(C2, 27 * C1)
     kf = fine_kernel.reshape(27 * C1, C1)
-    kc = coarse_kernel.reshape(27 * C2, C1)
-    any_spec = pl.BlockSpec(memory_space=pl.ANY)
+    kc = coarse_kernel.transpose(0, 1, 2, 4, 3).reshape(27 * C1, C2)
+    hbm = pl.BlockSpec(memory_space=pltpu.HBM)
     vmem = pl.BlockSpec(memory_space=pltpu.VMEM)
     dma = pltpu.SemaphoreType.DMA
     V = pltpu.VMEM
     tile = (8, 128)
-    outs = pl.pallas_call(
+    fine, coarse = (C1 * D * R, W), (C2 * HD * HR, HW)
+    parts = pl.pallas_call(
         kernel,
         out_shape=[
-            jax.ShapeDtypeStruct((C1 * D * R, W), BF16),
-            jax.ShapeDtypeStruct((C2 * HD * HR, HW), BF16),
-            jax.ShapeDtypeStruct((C1 * D * R, W), BF16),
-            jax.ShapeDtypeStruct((27, C1, C1), F32),
-            jax.ShapeDtypeStruct((27, C2, C1), F32),
+            jax.ShapeDtypeStruct(fine, BF16),
+            jax.ShapeDtypeStruct(coarse, BF16),
+            jax.ShapeDtypeStruct(fine, BF16),
+            jax.ShapeDtypeStruct((8, *tile), F32),
+            jax.ShapeDtypeStruct((16, *tile), F32),
         ],
-        in_specs=[any_spec] * 3 + [vmem] * 4,
+        in_specs=[hbm] * 5,
         out_specs=[vmem] * 5,
         scratch_shapes=[
-            V((C1 * D * R, W), BF16), V((C1 * D * R, W), BF16), V((C2 * HD * HR, HW), BF16),
-            V((2, C1 * D * R, 128), F32), V((2, C1 * D * R, 128), F32), V((C2 * HD * HR, HW), F32),
-            V((2, C1 * D * R, 128), F32), V((C2 * HD * HR, HW), F32),
+            V(fine, BF16), V(fine, BF16), V(coarse, BF16),
+            V((27 * C1, C1), BF16), V((27 * C1, C2), BF16),
+            V((2, C1 * D * R, 128), F32), V((2, C1 * D * R, 128), F32), V(coarse, F32),
+            V((2, C1 * D * R, 128), F32), V(coarse, F32),
             V((D + 2, R + 2, 3 * C1, W), BF16),
             V((HD + 2, HR + 2, C2, HW), BF16),
             V((HD + 4, HR + 4, 3 * C1, HW), BF16),
             V((HD + 2, HR + 2, 3 * C2, W), BF16),
             V((D + 2, R + 2, 3 * C1, W), BF16),
             V((D, R, C1, W), BF16), V((D, R, C1, W), F32), V((D, R, C1, W), F32),
-            V((HD + 2, HR + 2, C2, HW), BF16),
-            V((C1, 27 * C1), BF16), V((C1, 27 * C2), BF16),
+            V((HD + 2, HR + 2, C2, HW), BF16), V((HD + 2, HR, C2, HW), BF16),
+            V((C1, 27 * C1), F32), V((C1, 27 * C2), F32), V((C1, 27 * C1), BF16),
             V((8, *tile), F32), V((16, *tile), F32),
-            V((8, *tile), F32), V((16, *tile), F32), V((8, *tile), F32),
-            V((16, *tile), F32), V((8, *tile), F32), V((16, *tile), F32),
-            dma((3,)), dma((4, 8)), dma((4, 8)),
+            V((8, *tile), F32), V((16, *tile), F32),
+            V((16, *tile), F32), V((8, *tile), F32),
+            dma((5,)), dma((4, 8)), dma((4, 8)), pltpu.SemaphoreType.REGULAR((4, 2)),
             dma((8,)), dma((8,)), dma((16,)), dma((16,)), dma((8,)), dma((8,)),
             dma((16,)), dma((16,)), dma((8,)), dma((8,)), dma((16,)), dma((16,)),
         ],
@@ -489,18 +546,35 @@
         ),
         name="unet_levels",
     )(
-        volume.reshape(C1 * D * R, W),
-        fine_cotangent.reshape(C1 * D * R, W),
-        coarse_cotangent.reshape(C2 * HD * HR, HW),
-        wf, kf, wc, kc,
+        *(
+            pltpu.with_memory_space_constraint(value, pltpu.HBM)
+            for value in (
+                volume.reshape(fine), fine_cotangent.reshape(fine),
+                coarse_cotangent.reshape(coarse), kf, kc,
+            )
+        )
     )
-    fo, co, vg, fk, ck = outs
+    fo, co, vg, fk, ck = pl.pallas_call(
+        emit_kernel,
+        out_shape=[
+            jax.ShapeDtypeStruct(fine, BF16),
+            jax.ShapeDtypeStruct(coarse, BF16),
+            jax.ShapeDtypeStruct(fine, BF16),
+            jax.ShapeDtypeStruct((27, C1, C1), F32),
+            jax.ShapeDtypeStruct((27, C1, C2), F32),
+        ],
+        in_specs=[vmem] * 5,
+        out_specs=[hbm] * 5,
+        scratch_shapes=[V((27, C1, C1), F32), V((27, C1, C2), F32), dma((5,))],
+        compiler_params=pltpu.CompilerParams(vmem_limit_bytes=8 << 20),
+        name="emit",
+    )(*parts)
     return (
         fo.reshape(volume.shape),
         co.reshape(coarse_cotangent.shape),
         vg.reshape(volume.shape),
         fk.reshape(fine_kernel.shape),
-        ck.reshape(coarse_kernel.shape),
+        ck.reshape(3, 3, 3, C1, C2).transpose(0, 1, 2, 4, 3),
     )
 
 

time: 54.7 us -> 46.3 us (0.85)
  local copies, waits for them, and re-layouts: 6.32 us -> 0 us
  Pallas kernels: 47.4 us -> 45.6 us
    unnamed x16 -> x0, local copies, waits for them, and re-layouts: 5.13 us -> none
    pallas_call x1 -> x2, Pallas kernels: 47.4 us -> 45.6 us  [the longest x1 44.6 us: local(): pl.pallas_call(kernel, out_shape=[jax.ShapeDtypeStruct(fine, BF16), jax.S...]
    reshape x2 -> x0, local copies, waits for them, and re-layouts: 1.14 us -> none  [the longest x1 1.01 us: local(): wc = coarse_kernel.transpose(3, 0, 1, 2, 4).reshape(C2, 27 * C1)]
where the time goes in v2:
time: 46.3 us; the launch traced here: 46.2 us
  Pallas kernels  45.6 us (98%)
  between operations  0.64 us (1%)
    pallas_call x1, Pallas kernels, local(): pl.pallas_call(kernel, out_shape=[jax.ShapeDtypeStruct(fine, BF16), jax.S...  44.6 us
    pallas_call x1, Pallas kernels, local(): pl.pallas_call(emit_kernel, out_shape=[jax.ShapeDtypeStruct(fine, BF16),...  1 us

profile of v2, /device:TPU:1, one launch (start us, length us, event | category | flops | bytes accessed | tf_op | source)
XLA Modules:
  0.0 46.2 jit_solution(9325671883759574430)
XLA Ops:
  0.6 44.6 %unet_levels.1 = (bf16[512,256]{1,0:T(8,128)(2,1)S(1)}, bf16[256,128]{1,0:T(8,128)(2,1)S(1)}, bf16[512,256]{1,0:T(8,128)(2,1)S(1)}, f32[8,8,128]{2,1,0:T(8,128)S(1)}, f32[16,8,128]{2,1,0:T(8,128)S(1)}) custom-call(bf16[512,256]{1,0:T(8,128)(2,1)} %bitcast.14, bf16[512,256]{1,0:T(8,128)(2,1)} %bitcast.15, bf16[256,128]{1,0:T(8,128)(2,1)} %bitcast.18, ...), custom_call_target="tpu_custom_call" | custom-call | tf_op jit(solution)/shard_map/unet_levels/pallas_call | solution.py:513
  45.2 1.0 %emit.1 = (bf16[512,256]{1,0:T(8,128)(2,1)}, bf16[256,128]{1,0:T(8,128)(2,1)}, bf16[512,256]{1,0:T(8,128)(2,1)}, f32[27,16,16]{2,1,0:T(8,128)}, f32[27,16,32]{2,1,0:T(8,128)}) custom-call(bf16[512,256]{1,0:T(8,128)(2,1)S(1)} %get-tuple-element.15.fo, bf16[256,128]{1,0:T(8,128)(2,1)S(1)} %get-tuple-element.16.co, bf16[512,256]{1,0:T(8,128)(2,1)S(1)} %get-tuple-element.17.vg, ...), custom_call_target="tpu_custom_call" | custom-call | tf_op jit(solution)/shard_map/emit/pallas_call | solution.py:557

commit v3 on v2

--- a/solution.py
+++ b/solution.py
@@ -174,7 +174,7 @@
     vol_hbm, fcot_hbm, ccot_hbm, kf_hbm, kc_hbm,
     fo_ref, co_ref, vg_ref, ffin, cfin,
     raw_v, raw_f, raw_c, kf, kc, st_v, st_f, st_c, st_o, st_co,
-    vp, cp, qp, tp, sp, fob, g1, fg, csb, cob, w32, wc32, wft, ft, ct,
+    vp, cp, qp, tp, sp, fob, g1, fg, csb, cob, w32, wc32, wft, terms, ft, ct,
     frs, fbx, crs, cbx,
     in_sem, hs, hr, know, f_rs_s, f_rs_r, f_b_s, f_b_r, f_g_s, f_g_r,
     c_rs_s, c_rs_r, c_b_s, c_b_r, c_g_s, c_g_r,
@@ -386,28 +386,35 @@
         fo_ref[:, t * 128 : (t + 1) * 128] = st_o[t].astype(BF16)
     chalo.wait_recv()
     qhalo.wait_recv()
+    hear_word(1)
+    spread_word(2)
     halo_shifts(qp, 2, HD, HR, 1)
 
     @pl.loop(0, HD + 2)
     def _(z):
-        for y in range(HR + 2):
-            pre = dot(wc, taps(qp, z, y))
-            s = jax.nn.sigmoid(pre)
-            slope = cp[z, y].astype(F32) * (s * (1.0 + pre * (1.0 - s)))
-            csb[z, y] = slope.astype(BF16)
-            if 1 <= y <= HR:
-                cob[z, y - 1] = (pre * s).astype(BF16)
+        for y0 in range(0, HR + 2, 2):
+            pair = dot(wc, jnp.concatenate([taps(qp, z, y0), taps(qp, z, y0 + 1)], axis=1))
+            for y in (y0, y0 + 1):
+                pre = pair[:, (y - y0) * HW : (y - y0 + 1) * HW]
+                s = jax.nn.sigmoid(pre)
+                slope = cp[z, y].astype(F32) * (s * (1.0 + pre * (1.0 - s)))
+                csb[z, y] = slope.astype(BF16)
+                if 1 <= y <= HR:
+                    cob[z, y - 1] = (pre * s).astype(BF16)
         wide = dot(csb[z].reshape((HR + 2) * C2, HW), up_mat).astype(BF16)
         for c in range(3):
             tp[z, :, pl.ds(c * C2, C2), :] = wide[:, c * W : (c + 1) * W].reshape(HR + 2, C2, W)
 
-    hear_word(1)
-    spread_word(2)
-    ck = jnp.zeros((C2, 27 * C1), F32)
-    for z in range(HD):
-        for y in range(HR):
-            ck = ck + dot_nt(csb[z + 1, y + 1], taps(qp, z + 1, y + 1))
-    ck = jnp.concatenate([ck, jnp.zeros((C2, 80), F32)], axis=1)
+    def across(rows):
+        rows = jnp.concatenate([rows, jnp.zeros((80, rows.shape[1]), F32)], axis=0)
+        return jnp.transpose(rows)
+
+    cells = [(z + 1, y + 1) for z in range(HD) for y in range(HR)]
+    ck = dot_nt(
+        jnp.concatenate([taps(qp, *at) for at in cells], axis=1),
+        jnp.concatenate([csb[at] for at in cells], axis=1),
+    )
+    ck = across(ck)
     for i in range(4):
         for t in range(4):
             ct[i * 4 + t] = ck[i * 8 : (i + 1) * 8, t * 128 : (t + 1) * 128]
@@ -431,13 +438,16 @@
     hear_word(2)
     spread_word(3)
 
-    def fine_terms(z, acc):
-        for y in range(R):
-            acc = acc + dot_nt(sp[z + 1, y + 1, mid, :], taps(vp, z, y))
-        return acc
-
-    fk = lax.fori_loop(0, D, fine_terms, jnp.zeros((C1, 27 * C1), F32))
-    fk = jnp.concatenate([fk, jnp.zeros((C1, 80), F32)], axis=1)
+    terms[...] = jnp.zeros(terms.shape, F32)
+
+    @pl.loop(0, D)
+    def _(z):
+        slopes = jnp.concatenate([sp[z + 1, y + 1, mid, :] for y in range(R)], axis=1)
+        terms[...] += dot_nt(
+            jnp.concatenate([taps(vp, z, y) for y in range(R)], axis=1), slopes
+        )
+
+    fk = across(terms[...])
     for i in range(2):
         for t in range(4):
             ft[i * 4 + t] = fk[i * 8 : (i + 1) * 8, t * 128 : (t + 1) * 128]
@@ -464,12 +474,10 @@
         for y in range(HR):
             st_co[pl.ds(z * HR + y, C2, stride=HD * HR), :] = cob[z + 1, y].astype(F32)
     co_ref[...] = st_co[...].astype(BF16)
-    for one in (vhalo, chalo, qhalo, shalo):
+    for one in (vhalo, chalo, qhalo, shalo, c_sum, f_sum):
         one.wait_send()
     c_sum.finish()
     f_sum.finish()
-    for one in (c_sum, f_sum):
-        one.wait_send()
 
 
 def emit_kernel(fo, co, vg, ffin, cfin, fo_hbm, co_hbm, vg_hbm, fk_hbm, ck_hbm, fk, ck, sem):
@@ -533,7 +541,7 @@
             V((D + 2, R + 2, 3 * C1, W), BF16),
             V((D, R, C1, W), BF16), V((D, R, C1, W), F32), V((D, R, C1, W), F32),
             V((HD + 2, HR + 2, C2, HW), BF16), V((HD + 2, HR, C2, HW), BF16),
-            V((C1, 27 * C1), F32), V((C1, 27 * C2), F32), V((C1, 27 * C1), BF16),
+            V((C1, 27 * C1), F32), V((C1, 27 * C2), F32), V((C1, 27 * C1), BF16), V((27 * C1, C1), F32),
             V((8, *tile), F32), V((16, *tile), F32),
             V((8, *tile), F32), V((16, *tile), F32),
             V((16, *tile), F32), V((8, *tile), F32),

time: 46.3 us -> 44.2 us (0.955)
  Pallas kernels: 45.6 us -> 43.4 us
    pallas_call x1, Pallas kernels: 44.6 us -> 42.4 us  [local(): pl.pallas_call(kernel, out_shape=[jax.ShapeDtypeStruct(fine, BF16), jax.S...]
where the time goes in v3:
time: 44.2 us; the launch traced here: 44 us
  Pallas kernels  43.4 us (98%)
  between operations  0.64 us (1%)
    pallas_call x1, Pallas kernels, local(): pl.pallas_call(kernel, out_shape=[jax.ShapeDtypeStruct(fine, BF16), jax.S...  42.4 us
    pallas_call x1, Pallas kernels, local(): pl.pallas_call(emit_kernel, out_shape=[jax.ShapeDtypeStruct(fine, BF16),...  1 us

profile of v3, /device:TPU:1, one launch (start us, length us, event | category | flops | bytes accessed | tf_op | source)
XLA Modules:
  0.0 44.0 jit_solution(6637344437749773540)
XLA Ops:
  0.6 42.4 %unet_levels.1 = (bf16[512,256]{1,0:T(8,128)(2,1)S(1)}, bf16[256,128]{1,0:T(8,128)(2,1)S(1)}, bf16[512,256]{1,0:T(8,128)(2,1)S(1)}, f32[8,8,128]{2,1,0:T(8,128)S(1)}, f32[16,8,128]{2,1,0:T(8,128)S(1)}) custom-call(bf16[512,256]{1,0:T(8,128)(2,1)} %bitcast.14, bf16[512,256]{1,0:T(8,128)(2,1)} %bitcast.15, bf16[256,128]{1,0:T(8,128)(2,1)} %bitcast.18, ...), custom_call_target="tpu_custom_call" | custom-call | tf_op jit(solution)/shard_map/unet_levels/pallas_call | solution.py:521
  43.0 1.0 %emit.1 = (bf16[512,256]{1,0:T(8,128)(2,1)}, bf16[256,128]{1,0:T(8,128)(2,1)}, bf16[512,256]{1,0:T(8,128)(2,1)}, f32[27,16,16]{2,1,0:T(8,128)}, f32[27,16,32]{2,1,0:T(8,128)}) custom-call(bf16[512,256]{1,0:T(8,128)(2,1)S(1)} %get-tuple-element.15.fo, bf16[256,128]{1,0:T(8,128)(2,1)S(1)} %get-tuple-element.16.co, bf16[512,256]{1,0:T(8,128)(2,1)S(1)} %get-tuple-element.17.vg, ...), custom_call_target="tpu_custom_call" | custom-call | tf_op jit(solution)/shard_map/emit/pallas_call | solution.py:565

commit v4 on v3

--- a/solution.py
+++ b/solution.py
@@ -174,7 +174,8 @@
     vol_hbm, fcot_hbm, ccot_hbm, kf_hbm, kc_hbm,
     fo_ref, co_ref, vg_ref, ffin, cfin,
     raw_v, raw_f, raw_c, kf, kc, st_v, st_f, st_c, st_o, st_co,
-    vp, cp, qp, tp, sp, fob, g1, fg, csb, cob, w32, wc32, wft, terms, ft, ct,
+    vp, cp, qp, tp, sp, fob, g1, fg, csb, cob, w32, wc32, w32t, wc32n, packed,
+    wide_f, wide_t, wide_s, wide_c, band_f, band_t, band_s, band_c, ft, ct,
     frs, fbx, crs, cbx,
     in_sem, hs, hr, know, f_rs_s, f_rs_r, f_b_s, f_b_r, f_g_s, f_g_r,
     c_rs_s, c_rs_r, c_b_s, c_b_r, c_g_s, c_g_r,
@@ -314,7 +315,31 @@
         return (rows == lax.broadcasted_iota(jnp.int32, (n, n), 1)).astype(F32).astype(BF16)
 
     wf = w32[...].astype(BF16)
-    wft[...] = dot_nt(eye(C1), kf[...]).astype(BF16)
+    w32t[...] = dot_nt(eye(C1), kf[...])
+    wc32n[...] = dot_nt(eye(C2), kc[...])
+    for band in (wide_f, wide_t, wide_s, wide_c):
+        band[...] = jnp.zeros(band.shape, F32)
+    for a in range(3):
+        for r in range(4):
+            rows = pl.ds(r * C1, C1)
+            wide_f[rows, pl.ds(a * 288 + r * 48, 144)] = w32[:, a * 144 : (a + 1) * 144]
+            for b in range(3):
+                at = a * 3 + b
+                wide_t[rows, pl.ds(a * 288 + (r + 2 - b) * 48, 48)] = w32t[
+                    :, at * 48 : (at + 1) * 48
+                ]
+                wide_s[rows, pl.ds(a * 576 + (r + 2 - b) * 96, 96)] = wc32[
+                    :, at * 96 : (at + 1) * 96
+                ]
+        for r in range(2):
+            wide_c[pl.ds(r * C2, C2), pl.ds(a * 192 + r * 48, 144)] = wc32n[
+                :, a * 144 : (a + 1) * 144
+            ]
+    band_f[...] = wide_f[...].astype(BF16)
+    band_t[...] = wide_t[...].astype(BF16)
+    band_s[...] = wide_s[...].astype(BF16)
+    band_c[...] = wide_c[...].astype(BF16)
+    packed[...] = jnp.zeros(packed.shape, F32)
     loads[3].wait()
     st_c[...] = raw_c[...].astype(F32)
     for z in range(HD):
@@ -322,8 +347,20 @@
             cp[z + 1, y + 1] = st_c[pl.ds(z * HR + y, C2, stride=HD * HR), :].astype(BF16)
     chalo.start()
 
+    def block(buf, z, y, n):
+        return buf[z, pl.ds(y, n)].reshape(n * buf.shape[2], buf.shape[3])
+
+    def fine_band(z, y0):
+        four = dot(
+            band_f[...], jnp.concatenate([block(vp, z + a, y0, 6) for a in range(3)], axis=0)
+        )
+        for r in range(4):
+            fine_cell(z, y0 + r, four[r * C1 : (r + 1) * C1])
+
     def fine_row(z, y):
-        pre = dot(wf, taps(vp, z, y))
+        fine_cell(z, y, dot(wf, taps(vp, z, y)))
+
+    def fine_cell(z, y, pre):
         s = jax.nn.sigmoid(pre)
         out = (vp[z + 1, y + 1, mid, :].astype(F32) + pre * s).astype(BF16)
         g1[z, y] = s * (1.0 + pre * (1.0 - s))
@@ -334,8 +371,6 @@
         for y in range(1, R - 1):
             fine_row(z, y)
 
-    wc = dot_nt(eye(C2), kc[...]).astype(BF16)
-    wct = wc32[...].astype(BF16)
     pool_row = lax.broadcasted_iota(jnp.int32, (W, HW), 0)
     pool_col = lax.broadcasted_iota(jnp.int32, (W, HW), 1)
     pool_mat = (lax.div(pool_row, 2) == pool_col).astype(F32).astype(BF16)
@@ -353,8 +388,8 @@
 
     @pl.loop(0, 2)
     def _(side):
-        for y in range(R):
-            fine_row(side * (D - 1), y)
+        for y in (0, 4):
+            fine_band(side * (D - 1), y)
         for y in (0, R - 1):
             fine_row(side + 1, y)
 
@@ -390,20 +425,30 @@
     spread_word(2)
     halo_shifts(qp, 2, HD, HR, 1)
 
-    @pl.loop(0, HD + 2)
-    def _(z):
+    @pl.loop(0, HD)
+    def _(zp):
         for y0 in range(0, HR + 2, 2):
-            pair = dot(wc, jnp.concatenate([taps(qp, z, y0), taps(qp, z, y0 + 1)], axis=1))
-            for y in (y0, y0 + 1):
-                pre = pair[:, (y - y0) * HW : (y - y0 + 1) * HW]
-                s = jax.nn.sigmoid(pre)
-                slope = cp[z, y].astype(F32) * (s * (1.0 + pre * (1.0 - s)))
-                csb[z, y] = slope.astype(BF16)
-                if 1 <= y <= HR:
-                    cob[z, y - 1] = (pre * s).astype(BF16)
-        wide = dot(csb[z].reshape((HR + 2) * C2, HW), up_mat).astype(BF16)
-        for c in range(3):
-            tp[z, :, pl.ds(c * C2, C2), :] = wide[:, c * W : (c + 1) * W].reshape(HR + 2, C2, W)
+            two = [
+                jnp.concatenate([block(qp, zp * 2 + k + a, y0, 4) for a in range(3)], axis=0)
+                for k in range(2)
+            ]
+            pair = dot(band_c[...], jnp.concatenate(two, axis=1))
+            for r in range(2):
+                for k in range(2):
+                    z, y = zp * 2 + k, y0 + r
+                    pre = pair[r * C2 : (r + 1) * C2, k * HW : (k + 1) * HW]
+                    s = jax.nn.sigmoid(pre)
+                    slope = cp[z, y].astype(F32) * (s * (1.0 + pre * (1.0 - s)))
+                    csb[z, y] = slope.astype(BF16)
+                    if 1 <= y <= HR:
+                        cob[z, y - 1] = (pre * s).astype(BF16)
+        for k in range(2):
+            z = zp * 2 + k
+            wide = dot(csb[z].reshape((HR + 2) * C2, HW), up_mat).astype(BF16)
+            for c in range(3):
+                tp[z, :, pl.ds(c * C2, C2), :] = wide[:, c * W : (c + 1) * W].reshape(
+                    HR + 2, C2, W
+                )
 
     def across(rows):
         rows = jnp.concatenate([rows, jnp.zeros((80, rows.shape[1]), F32)], axis=0)
@@ -422,8 +467,11 @@
 
     @pl.loop(0, HD)
     def _(zc):
+        four = dot(
+            band_s[...], jnp.concatenate([block(tp, zc + 2 - a, 0, 6) for a in range(3)], axis=0)
+        )
         for yc in range(HR):
-            spread = dot(wct, taps(tp, zc, yc, True)) * 0.125
+            spread = four[yc * C1 : (yc + 1) * C1] * 0.125
             for zz in range(2):
                 for yy in range(2):
                     z, y = zc * 2 + zz, yc * 2 + yy
@@ -438,16 +486,30 @@
     hear_word(2)
     spread_word(3)
 
-    terms[...] = jnp.zeros(terms.shape, F32)
-
-    @pl.loop(0, D)
-    def _(z):
-        slopes = jnp.concatenate([sp[z + 1, y + 1, mid, :] for y in range(R)], axis=1)
-        terms[...] += dot_nt(
-            jnp.concatenate([taps(vp, z, y) for y in range(R)], axis=1), slopes
-        )
-
-    fk = across(terms[...])
+    def slope_rows(z, yb):
+        if not 0 <= z < D:
+            return jnp.zeros((4 * C1, W), BF16)
+        return sp[z + 1, pl.ds(yb * 4 + 1, 4), mid, :].reshape(4 * C1, W)
+
+    steps = [(z, yb) for z in range(D + 2) for yb in range(2)]
+    pairs = dot_nt(
+        jnp.concatenate([block(vp, z, yb * 4, 6) for z, yb in steps], axis=1),
+        jnp.concatenate(
+            [
+                jnp.concatenate([slope_rows(z - a, yb) for a in range(3)], axis=0)
+                for z, yb in steps
+            ],
+            axis=1,
+        ),
+    )
+    pairs = jnp.concatenate([pairs, jnp.zeros((288, 64), F32)], axis=1)
+    pairs = jnp.transpose(jnp.concatenate([pairs, jnp.zeros((96, 256), F32)], axis=0))
+    for a in range(3):
+        total = pairs[a * 64 : a * 64 + 16, 0:144]
+        for y in range(1, 4):
+            total = total + pairs[a * 64 + y * 16 : a * 64 + y * 16 + 16, y * 48 : y * 48 + 144]
+        packed[:, a * 144 : (a + 1) * 144] = total
+    fk = packed[...]
     for i in range(2):
         for t in range(4):
             ft[i * 4 + t] = fk[i * 8 : (i + 1) * 8, t * 128 : (t + 1) * 128]
@@ -458,12 +520,16 @@
     f_sum.start_exchange()
     shalo.wait_recv()
     halo_shifts(sp, 1, D, R, -1)
-    wft_v = wft[...]
 
     @pl.loop(0, D)
     def _(z):
-        for y in range(R):
-            fg[z, y] = fg[z, y] + dot(wft_v, taps(sp, z, y, True))
+        for y0 in (0, 4):
+            four = dot(
+                band_t[...],
+                jnp.concatenate([block(sp, z + 2 - a, y0, 6) for a in range(3)], axis=0),
+            )
+            for r in range(4):
+                fg[z, y0 + r] = fg[z, y0 + r] + four[r * C1 : (r + 1) * C1]
 
     c_sum.start_gather()
     f_sum.start_gather()
@@ -541,7 +607,10 @@
             V((D + 2, R + 2, 3 * C1, W), BF16),
             V((D, R, C1, W), BF16), V((D, R, C1, W), F32), V((D, R, C1, W), F32),
             V((HD + 2, HR + 2, C2, HW), BF16), V((HD + 2, HR, C2, HW), BF16),
-            V((C1, 27 * C1), F32), V((C1, 27 * C2), F32), V((C1, 27 * C1), BF16), V((27 * C1, C1), F32),
+            V((C1, 27 * C1), F32), V((C1, 27 * C2), F32),
+            V((C1, 27 * C1), F32), V((C2, 27 * C1), F32), V((C1, 512), F32),
+            V((64, 864), F32), V((64, 864), F32), V((64, 1728), F32), V((64, 576), F32),
+            V((64, 864), BF16), V((64, 864), BF16), V((64, 1728), BF16), V((64, 576), BF16),
             V((8, *tile), F32), V((16, *tile), F32),
             V((8, *tile), F32), V((16, *tile), F32),
             V((16, *tile), F32), V((8, *tile), F32),

time: 44.2 us -> 42.3 us (0.957)
  Pallas kernels: 43.4 us -> 41.5 us
    pallas_call x1, Pallas kernels: 42.4 us -> 40.5 us  [local(): pl.pallas_call(kernel, out_shape=[jax.ShapeDtypeStruct(fine, BF16), jax.S...]
where the time goes in v4:
time: 42.3 us; the launch traced here: 42.2 us
  Pallas kernels  41.5 us (98%)
  between operations  0.64 us (2%)
    pallas_call x1, Pallas kernels, local(): pl.pallas_call(kernel, out_shape=[jax.ShapeDtypeStruct(fine, BF16), jax.S...  40.5 us
    pallas_call x1, Pallas kernels, local(): pl.pallas_call(emit_kernel, out_shape=[jax.ShapeDtypeStruct(fine, BF16),...  1 us

profile of v4, /device:TPU:1, one launch (start us, length us, event | category | flops | bytes accessed | tf_op | source)
XLA Modules:
  0.0 42.2 jit_solution(4266414592725140170)
XLA Ops:
  0.6 40.5 %unet_levels.1 = (bf16[512,256]{1,0:T(8,128)(2,1)S(1)}, bf16[256,128]{1,0:T(8,128)(2,1)S(1)}, bf16[512,256]{1,0:T(8,128)(2,1)S(1)}, f32[8,8,128]{2,1,0:T(8,128)S(1)}, f32[16,8,128]{2,1,0:T(8,128)S(1)}) custom-call(bf16[512,256]{1,0:T(8,128)(2,1)} %bitcast.14, bf16[512,256]{1,0:T(8,128)(2,1)} %bitcast.15, bf16[256,128]{1,0:T(8,128)(2,1)} %bitcast.18, ...), custom_call_target="tpu_custom_call" | custom-call | tf_op jit(solution)/shard_map/unet_levels/pallas_call | solution.py:587
  41.2 1.0 %emit.1 = (bf16[512,256]{1,0:T(8,128)(2,1)}, bf16[256,128]{1,0:T(8,128)(2,1)}, bf16[512,256]{1,0:T(8,128)(2,1)}, f32[27,16,16]{2,1,0:T(8,128)}, f32[27,16,32]{2,1,0:T(8,128)}) custom-call(bf16[512,256]{1,0:T(8,128)(2,1)S(1)} %get-tuple-element.15.fo, bf16[256,128]{1,0:T(8,128)(2,1)S(1)} %get-tuple-element.16.co, bf16[512,256]{1,0:T(8,128)(2,1)S(1)} %get-tuple-element.17.vg, ...), custom_call_target="tpu_custom_call" | custom-call | tf_op jit(solution)/shard_map/emit/pallas_call | solution.py:634

commit v5 on v4

--- a/solution.py
+++ b/solution.py
@@ -12,7 +12,7 @@
 D, R, W = 4, 8, 256
 HD, HR, HW = 2, 4, 128
 NGX, NGY = 32, 4
-DIRS = [(sx, sy) for sx in (-1, 0, 1) for sy in (-1, 0, 1) if (sx, sy) != (0, 0)]
+DIRS = [(-1, -1), (-1, 1), (1, -1), (1, 1), (-1, 0), (1, 0), (0, -1), (0, 1)]
 NT = (((1,), (1,)), ((), ()))
 
 
@@ -94,8 +94,9 @@
             def _(i=i):
                 self.desc(i).start()
 
-    def wait_recv(self):
-        for i, (sx, sy) in enumerate(DIRS):
+    def wait_recv(self, chosen=range(8)):
+        for i in chosen:
+            sx, sy = DIRS[i]
 
             @pl.when(exists(self.gx, self.gy, -sx, -sy))
             def _(i=i):
@@ -107,6 +108,44 @@
             @pl.when(exists(self.gx, self.gy, sx, sy))
             def _(i=i):
                 self.desc(i).wait_send()
+
+
+class PlaneHalo(Halo):
+    def plane(self, p, i):
+        sx, sy = DIRS[i]
+        y0, yn = span(sy, self.h, self.ny, True)
+        y1, _ = span(sy, self.h, self.ny, False)
+        return pltpu.make_async_remote_copy(
+            src_ref=self.buf.at[pl.ds(p + self.h, 1), pl.ds(y0, yn), self.chan, :],
+            dst_ref=self.buf.at[pl.ds(p + self.h - 2 * sx, 1), pl.ds(y1, yn), self.chan, :],
+            send_sem=self.send_sem.at[p, i],
+            recv_sem=self.recv_sem.at[p, i],
+            device_id=(self.gx + sx, self.gy + sy),
+            device_id_type=MESH,
+        )
+
+    def start(self, p):
+        for i, (sx, sy) in enumerate(DIRS):
+
+            @pl.when(exists(self.gx, self.gy, sx, sy))
+            def _(i=i):
+                self.plane(p, i).start()
+
+    def wait_recv(self):
+        for i, (sx, sy) in enumerate(DIRS):
+
+            @pl.when(exists(self.gx, self.gy, -sx, -sy))
+            def _(i=i):
+                for p in range(2):
+                    self.plane(p, i).wait_recv()
+
+    def wait_send(self):
+        for i, (sx, sy) in enumerate(DIRS):
+
+            @pl.when(exists(self.gx, self.gy, sx, sy))
+            def _(i=i):
+                for p in range(2):
+                    self.plane(p, i).wait_send()
 
 
 class AllReduce:
@@ -177,7 +216,7 @@
     vp, cp, qp, tp, sp, fob, g1, fg, csb, cob, w32, wc32, w32t, wc32n, packed,
     wide_f, wide_t, wide_s, wide_c, band_f, band_t, band_s, band_c, ft, ct,
     frs, fbx, crs, cbx,
-    in_sem, hs, hr, know, f_rs_s, f_rs_r, f_b_s, f_b_r, f_g_s, f_g_r,
+    in_sem, hs, hr, qs, qr, know, f_rs_s, f_rs_r, f_b_s, f_b_r, f_g_s, f_g_r,
     c_rs_s, c_rs_r, c_b_s, c_b_r, c_g_s, c_g_r,
 ):
     gx, gy = lax.axis_index("gx"), lax.axis_index("gy")
@@ -194,6 +233,15 @@
                 barrier, inc=1, device_id=(gx + sx, gy + sy), device_id_type=MESH
             )
 
+    zi, hi = lax.rem(gx, 4), lax.div(gx, 4)
+    ring = [lax.div(hi, 4) * 16 + lax.rem(hi + k, 4) * 4 + zi for k in (1, 3)]
+    across = lax.rem(gx + 16, NGX)
+    for far in (*ring, across):
+        pl.semaphore_signal(barrier, inc=1, device_id=(far, gy), device_id_type=MESH)
+
+    def tell(one, device):
+        pl.semaphore_signal(know.at[one], inc=1, device_id=(device, gy), device_id_type=MESH)
+
     loads = [
         pltpu.make_async_copy(src, dst, in_sem.at[i])
         for i, (src, dst) in enumerate(
@@ -206,7 +254,6 @@
     for load in loads:
         load.start()
 
-    zi, hi = lax.rem(gx, 4), lax.div(gx, 4)
     y_lo, core = lax.div(gy, 2), lax.rem(gy, 2)
     base = hi * 4
 
@@ -224,28 +271,17 @@
 
     a_c, a_f, b_f = zi * 4 + gy, zi * 2 + core, hi * 2 + y_lo
 
-    def spread_word(step):
-        reach = 2 << step
-        for side, sign in enumerate((1, -1)):
-
-            @pl.when((gx < NGX - reach) if sign == 1 else (gx >= reach))
-            def _(side=side, sign=sign):
-                pl.semaphore_signal(
-                    know.at[step, side], inc=1,
-                    device_id=(gx + sign * reach, gy), device_id_type=MESH,
-                )
-
-    def hear_word(step):
-        reach = 2 << step
-        for side, sign in enumerate((1, -1)):
-
-            @pl.when((gx >= reach) if sign == 1 else (gx < NGX - reach))
-            def _(side=side):
-                pl.semaphore_wait(know.at[step, side], 1)
+    def hear_ring():
+        for one in range(2):
+            pl.semaphore_wait(know.at[one], 1)
+        tell(2, across)
+
+    def hear_across():
+        pl.semaphore_wait(know.at[2], 1)
 
     vhalo = Halo(vp, mid, 1, D, R, hs.at[0], hr.at[0], gx, gy)
     chalo = Halo(cp, slice(None), 1, HD, HR, hs.at[1], hr.at[1], gx, gy)
-    qhalo = Halo(qp, mid, 2, HD, HR, hs.at[2], hr.at[2], gx, gy)
+    qhalo = PlaneHalo(qp, mid, 2, HD, HR, qs, qr, gx, gy)
     shalo = Halo(sp, mid, 1, D, R, hs.at[3], hr.at[3], gx, gy)
     f_sum = AllReduce(
         ft, frs, fbx, ffin, (f_rs_s, f_rs_r, f_b_s, f_b_r, f_g_s, f_g_r),
@@ -267,8 +303,10 @@
                 vp[z + 1, y + 1, mid, pl.ds(t * 128, 128)] = st_v[
                     t, pl.ds(z * R + y, C1, stride=D * R), :
                 ].astype(BF16)
-    pl.semaphore_wait(barrier, n_halo)
+    pl.semaphore_wait(barrier, n_halo + 3)
     vhalo.start()
+    for one in range(2):
+        tell(one, ring[one])
 
     def put_shifts(buf, z, y, order):
         before, after = shifted(buf[z, y, mid, :].astype(F32))
@@ -382,29 +420,39 @@
     loads[4].wait()
     for t in range(2):
         st_f[t] = raw_f[:, t * 128 : (t + 1) * 128].astype(F32)
-    vhalo.wait_recv()
-    spread_word(0)
-    halo_shifts(vp, 1, D, R, 1)
-
-    @pl.loop(0, 2)
-    def _(side):
+    vhalo.wait_recv((6, 7))
+
+    @pl.loop(0, D)
+    def _(z):
+        for y in (0, R + 1):
+            put_shifts(vp, z + 1, y, 1)
+
+    late = (zi == 0).astype(jnp.int32)
+    for side in (late, 1 - late):
+
+        @pl.when(side == 0)
+        def _():
+            vhalo.wait_recv((2, 3, 5))
+
+        @pl.when(side == 1)
+        def _():
+            vhalo.wait_recv((0, 1, 4))
+
+        for y in range(R + 2):
+            put_shifts(vp, side * (D + 1), y, 1)
         for y in (0, 4):
             fine_band(side * (D - 1), y)
         for y in (0, R - 1):
             fine_row(side + 1, y)
-
-    @pl.loop(0, HD)
-    def _(zc):
         for yc in range(HR):
-            four = fob[pl.ds(zc * 2, 2), pl.ds(yc * 2, 2)].reshape(4 * C1, W)
+            four = fob[pl.ds(side * 2, 2), pl.ds(yc * 2, 2)].reshape(4 * C1, W)
             half = dot(four, pool_mat)
             total = half[0:16] + half[16:32] + half[32:48] + half[48:64]
-            qp[zc + 2, yc + 2, mid, :] = (total * 0.125).astype(BF16)
-
-    qhalo.start()
+            qp[side + 2, yc + 2, mid, :] = (total * 0.125).astype(BF16)
+        qhalo.start(side)
+
+    hear_ring()
     own_shifts(qp, 2, HD, HR, 1)
-    hear_word(0)
-    spread_word(1)
 
     def rows_out(rows, store):
         @pl.loop(0, D)
@@ -421,8 +469,7 @@
         fo_ref[:, t * 128 : (t + 1) * 128] = st_o[t].astype(BF16)
     chalo.wait_recv()
     qhalo.wait_recv()
-    hear_word(1)
-    spread_word(2)
+    hear_across()
     halo_shifts(qp, 2, HD, HR, 1)
 
     @pl.loop(0, HD)
@@ -450,7 +497,7 @@
                     HR + 2, C2, W
                 )
 
-    def across(rows):
+    def turned(rows):
         rows = jnp.concatenate([rows, jnp.zeros((80, rows.shape[1]), F32)], axis=0)
         return jnp.transpose(rows)
 
@@ -459,7 +506,7 @@
         jnp.concatenate([taps(qp, *at) for at in cells], axis=1),
         jnp.concatenate([csb[at] for at in cells], axis=1),
     )
-    ck = across(ck)
+    ck = turned(ck)
     for i in range(4):
         for t in range(4):
             ct[i * 4 + t] = ck[i * 8 : (i + 1) * 8, t * 128 : (t + 1) * 128]
@@ -483,8 +530,6 @@
                     sp[z + 1, y + 1, mid, :] = (grad * g1[z, y]).astype(BF16)
 
     shalo.start()
-    hear_word(2)
-    spread_word(3)
 
     def slope_rows(z, yb):
         if not 0 <= z < D:
@@ -514,7 +559,6 @@
         for t in range(4):
             ft[i * 4 + t] = fk[i * 8 : (i + 1) * 8, t * 128 : (t + 1) * 128]
     f_sum.start_scatter()
-    hear_word(3)
     c_sum.start_exchange()
     own_shifts(sp, 1, D, R, -1)
     f_sum.start_exchange()
@@ -614,7 +658,7 @@
             V((8, *tile), F32), V((16, *tile), F32),
             V((8, *tile), F32), V((16, *tile), F32),
             V((16, *tile), F32), V((8, *tile), F32),
-            dma((5,)), dma((4, 8)), dma((4, 8)), pltpu.SemaphoreType.REGULAR((4, 2)),
+            dma((5,)), dma((4, 8)), dma((4, 8)), dma((2, 8)), dma((2, 8)), pltpu.SemaphoreType.REGULAR((3,)),
             dma((8,)), dma((8,)), dma((16,)), dma((16,)), dma((8,)), dma((8,)),
             dma((16,)), dma((16,)), dma((8,)), dma((8,)), dma((16,)), dma((16,)),
         ],

time: 42.3 us -> 41 us (0.969)
  Pallas kernels: 41.5 us -> 40.2 us
    pallas_call x1, Pallas kernels: 40.5 us -> 39.2 us  [local(): pl.pallas_call(kernel, out_shape=[jax.ShapeDtypeStruct(fine, BF16), jax.S...]
where the time goes in v5:
time: 41 us; the launch traced here: 40.9 us
  Pallas kernels  40.2 us (98%)
  between operations  0.64 us (2%)
    pallas_call x1, Pallas kernels, local(): pl.pallas_call(kernel, out_shape=[jax.ShapeDtypeStruct(fine, BF16), jax.S...  39.2 us
    pallas_call x1, Pallas kernels, local(): pl.pallas_call(emit_kernel, out_shape=[jax.ShapeDtypeStruct(fine, BF16),...  1 us

profile of v5, /device:TPU:1, one launch (start us, length us, event | category | flops | bytes accessed | tf_op | source)
XLA Modules:
  0.0 40.9 jit_solution(9336834455513430293)
XLA Ops:
  0.6 39.2 %unet_levels.1 = (bf16[512,256]{1,0:T(8,128)(2,1)S(1)}, bf16[256,128]{1,0:T(8,128)(2,1)S(1)}, bf16[512,256]{1,0:T(8,128)(2,1)S(1)}, f32[8,8,128]{2,1,0:T(8,128)S(1)}, f32[16,8,128]{2,1,0:T(8,128)S(1)}) custom-call(bf16[512,256]{1,0:T(8,128)(2,1)} %bitcast.14, bf16[512,256]{1,0:T(8,128)(2,1)} %bitcast.15, bf16[256,128]{1,0:T(8,128)(2,1)} %bitcast.18, ...), custom_call_target="tpu_custom_call" | custom-call | tf_op jit(solution)/shard_map/unet_levels/pallas_call | solution.py:631
  39.9 1.0 %emit.1 = (bf16[512,256]{1,0:T(8,128)(2,1)}, bf16[256,128]{1,0:T(8,128)(2,1)}, bf16[512,256]{1,0:T(8,128)(2,1)}, f32[27,16,16]{2,1,0:T(8,128)}, f32[27,16,32]{2,1,0:T(8,128)}) custom-call(bf16[512,256]{1,0:T(8,128)(2,1)S(1)} %get-tuple-element.15.fo, bf16[256,128]{1,0:T(8,128)(2,1)S(1)} %get-tuple-element.16.co, bf16[512,256]{1,0:T(8,128)(2,1)S(1)} %get-tuple-element.17.vg, ...), custom_call_target="tpu_custom_call" | custom-call | tf_op jit(solution)/shard_map/emit/pallas_call | solution.py:678

commit v6 on v5

--- a/solution.py
+++ b/solution.py
@@ -131,8 +131,9 @@
             def _(i=i):
                 self.plane(p, i).start()
 
-    def wait_recv(self):
-        for i, (sx, sy) in enumerate(DIRS):
+    def wait_recv(self, chosen):
+        for i in chosen:
+            sx, sy = DIRS[i]
 
             @pl.when(exists(self.gx, self.gy, -sx, -sy))
             def _(i=i):
@@ -468,12 +469,26 @@
     for t in range(2):
         fo_ref[:, t * 128 : (t + 1) * 128] = st_o[t].astype(BF16)
     chalo.wait_recv()
-    qhalo.wait_recv()
-    hear_across()
-    halo_shifts(qp, 2, HD, HR, 1)
+    qhalo.wait_recv((6, 7))
 
     @pl.loop(0, HD)
-    def _(zp):
+    def _(z):
+        for y in (0, 1, HR + 2, HR + 3):
+            put_shifts(qp, z + 2, y, 1)
+
+    for zp in (late, 1 - late):
+
+        @pl.when(zp == 0)
+        def _():
+            qhalo.wait_recv((2, 3, 5))
+
+        @pl.when(zp == 1)
+        def _():
+            qhalo.wait_recv((0, 1, 4))
+
+        for k in range(2):
+            for y in range(HR + 4):
+                put_shifts(qp, zp * 4 + k, y, 1)
         for y0 in range(0, HR + 2, 2):
             two = [
                 jnp.concatenate([block(qp, zp * 2 + k + a, y0, 4) for a in range(3)], axis=0)
@@ -496,6 +511,8 @@
                 tp[z, :, pl.ds(c * C2, C2), :] = wide[:, c * W : (c + 1) * W].reshape(
                     HR + 2, C2, W
                 )
+
+    hear_across()
 
     def turned(rows):
         rows = jnp.concatenate([rows, jnp.zeros((80, rows.shape[1]), F32)], axis=0)

time: 41 us -> 40.1 us (0.978)
  Pallas kernels: 40.2 us -> 39.4 us
    pallas_call x1, Pallas kernels: 39.2 us -> 38.4 us  [local(): pl.pallas_call(kernel, out_shape=[jax.ShapeDtypeStruct(fine, BF16), jax.S...]
where the time goes in v6:
time: 40.1 us; the launch traced here: 40 us
  Pallas kernels  39.4 us (98%)
  between operations  0.64 us (2%)
    pallas_call x1, Pallas kernels, local(): pl.pallas_call(kernel, out_shape=[jax.ShapeDtypeStruct(fine, BF16), jax.S...  38.4 us
    pallas_call x1, Pallas kernels, local(): pl.pallas_call(emit_kernel, out_shape=[jax.ShapeDtypeStruct(fine, BF16),...  1 us

profile of v6, /device:TPU:1, one launch (start us, length us, event | category | flops | bytes accessed | tf_op | source)
XLA Modules:
  0.0 40.0 jit_solution(13434921972394313294)
XLA Ops:
  0.6 38.4 %unet_levels.1 = (bf16[512,256]{1,0:T(8,128)(2,1)S(1)}, bf16[256,128]{1,0:T(8,128)(2,1)S(1)}, bf16[512,256]{1,0:T(8,128)(2,1)S(1)}, f32[8,8,128]{2,1,0:T(8,128)S(1)}, f32[16,8,128]{2,1,0:T(8,128)S(1)}) custom-call(bf16[512,256]{1,0:T(8,128)(2,1)} %bitcast.14, bf16[512,256]{1,0:T(8,128)(2,1)} %bitcast.15, bf16[256,128]{1,0:T(8,128)(2,1)} %bitcast.18, ...), custom_call_target="tpu_custom_call" | custom-call | tf_op jit(solution)/shard_map/unet_levels/pallas_call | solution.py:648
  39.0 1.0 %emit.1 = (bf16[512,256]{1,0:T(8,128)(2,1)}, bf16[256,128]{1,0:T(8,128)(2,1)}, bf16[512,256]{1,0:T(8,128)(2,1)}, f32[27,16,16]{2,1,0:T(8,128)}, f32[27,16,32]{2,1,0:T(8,128)}) custom-call(bf16[512,256]{1,0:T(8,128)(2,1)S(1)} %get-tuple-element.15.fo, bf16[256,128]{1,0:T(8,128)(2,1)S(1)} %get-tuple-element.16.co, bf16[512,256]{1,0:T(8,128)(2,1)S(1)} %get-tuple-element.17.vg, ...), custom_call_target="tpu_custom_call" | custom-call | tf_op jit(solution)/shard_map/emit/pallas_call | solution.py:695

commit v7 on v6

--- a/solution.py
+++ b/solution.py
@@ -579,6 +579,8 @@
     c_sum.start_exchange()
     own_shifts(sp, 1, D, R, -1)
     f_sum.start_exchange()
+    c_sum.start_gather()
+    f_sum.start_gather()
     shalo.wait_recv()
     halo_shifts(sp, 1, D, R, -1)
 
@@ -592,8 +594,6 @@
             for r in range(4):
                 fg[z, y0 + r] = fg[z, y0 + r] + four[r * C1 : (r + 1) * C1]
 
-    c_sum.start_gather()
-    f_sum.start_gather()
     rows_out(fg, st_o)
     for t in range(2):
         vg_ref[:, t * 128 : (t + 1) * 128] = st_o[t].astype(BF16)

time: 40.1 us -> 40.1 us (level)
  no operation moved by 1% of the time
where the time goes in v7:
time: 40.1 us; the launch traced here: 40 us
  Pallas kernels  39.4 us (98%)
  between operations  0.64 us (2%)
    pallas_call x1, Pallas kernels, local(): pl.pallas_call(kernel, out_shape=[jax.ShapeDtypeStruct(fine, BF16), jax.S...  38.4 us
    pallas_call x1, Pallas kernels, local(): pl.pallas_call(emit_kernel, out_shape=[jax.ShapeDtypeStruct(fine, BF16),...  1 us

profile of v7, /device:TPU:1, one launch (start us, length us, event | category | flops | bytes accessed | tf_op | source)
XLA Modules:
  0.0 40.0 jit_solution(16037744431403540436)
XLA Ops:
  0.6 38.4 %unet_levels.1 = (bf16[512,256]{1,0:T(8,128)(2,1)S(1)}, bf16[256,128]{1,0:T(8,128)(2,1)S(1)}, bf16[512,256]{1,0:T(8,128)(2,1)S(1)}, f32[8,8,128]{2,1,0:T(8,128)S(1)}, f32[16,8,128]{2,1,0:T(8,128)S(1)}) custom-call(bf16[512,256]{1,0:T(8,128)(2,1)} %bitcast.14, bf16[512,256]{1,0:T(8,128)(2,1)} %bitcast.15, bf16[256,128]{1,0:T(8,128)(2,1)} %bitcast.18, ...), custom_call_target="tpu_custom_call" | custom-call | tf_op jit(solution)/shard_map/unet_levels/pallas_call | solution.py:648
  39.0 1.0 %emit.1 = (bf16[512,256]{1,0:T(8,128)(2,1)}, bf16[256,128]{1,0:T(8,128)(2,1)}, bf16[512,256]{1,0:T(8,128)(2,1)}, f32[27,16,16]{2,1,0:T(8,128)}, f32[27,16,32]{2,1,0:T(8,128)}) custom-call(bf16[512,256]{1,0:T(8,128)(2,1)S(1)} %get-tuple-element.15.fo, bf16[256,128]{1,0:T(8,128)(2,1)S(1)} %get-tuple-element.16.co, bf16[512,256]{1,0:T(8,128)(2,1)S(1)} %get-tuple-element.17.vg, ...), custom_call_target="tpu_custom_call" | custom-call | tf_op jit(solution)/shard_map/emit/pallas_call | solution.py:695
